TPU v7x, 256 devices: a whole 4x4x8 slice. The times are simulated.
256 devices in a mesh: row: 32 (over y, z), col: 8 (over x, core).
Axes of the slice: x: 4, y: 4, z: 8, core: 2. Of those that a mesh axis runs over, the one named last changes fastest.
Arguments:
- panel: float32 [8, 32, 256, 256], P(None, 'row', None, 'col'), may hold values from -0.1875 to 0.1875
- slab: bfloat16 [8, 32, 256, 4, 8, 256], P(None, 'row', None, None, 'col'), may hold values from -6 to 6
- cotangent: bfloat16 [8, 32, 256, 4, 8, 256], P(None, 'row', None, None, 'col'), may hold values from -0.0625 to 0.0625
- inverse: float32 [256, 256], replicated, may hold values from -2 to 8, as said below
Outputs:
- updated: bfloat16 [8, 32, 256, 4, 8, 256], P(None, 'row', None, None, 'col')
- grad_panel: float32 [8, 32, 256, 256], P(None, 'row', None, 'col')
- grad_inverse: float32 [256, 256], P(None, 'col')
Inputs may be any that keep to these rules, and one draw needn't show every extreme that they name: `inverse`: lower triangular; diagonal entries between 4 and 8.
All inputs are finite; a program needn't handle non-finite values.
Results may differ from a plain program's by a relative error of at most 0.015.
Values may be sent and summed in bfloat16 or wider, within the bound.
A program may use at most 128 MiB of HBM per device.

v0:
```python
import jax
import jax.numpy as jnp
from jax import lax
from jax.sharding import PartitionSpec as P


def per_device(panel, slab, cotangent, inverse):
    tiles_local = panel.shape[0]
    tile_size = panel.shape[2]
    strip_width = panel.shape[3]
    slab_tiles = slab.shape[3]
    row_count = tiles_local * tile_size
    slab_width = slab_tiles * tile_size
    row_devices = lax.axis_size("row")
    col_devices = lax.axis_size("col")
    row_index = lax.axis_index("row")
    col_index = lax.axis_index("col")
    highest = lax.Precision.HIGHEST
    contract_rows = (((0,), (0,)), ((), ()))
    panel_rows = panel.reshape(row_count, strip_width)
    gathered = lax.all_gather(panel_rows, "col", axis=1, tiled=True)
    factor = jnp.dot(gathered, inverse.T, precision=highest, preferred_element_type=jnp.float32)
    rounded = factor.astype(jnp.bfloat16)
    factor_tiles = rounded.reshape(tiles_local, tile_size, tile_size)
    tile_list = []
    for column_slot in range(slab_tiles):
        tile_index = column_slot * col_devices + col_index
        is_owner = tile_index % row_devices == row_index
        owned_tile = lax.dynamic_index_in_dim(
            factor_tiles, tile_index // row_devices, 0, keepdims=False
        )
        tile_list.append(jnp.where(is_owner, owned_tile, jnp.zeros_like(owned_tile)))
    stacked = jnp.stack(tile_list).reshape(slab_width, tile_size)
    slab_factor = lax.psum(stacked, "row").astype(jnp.float32).astype(jnp.bfloat16)
    slab_rows = slab.reshape(row_count, slab_width)
    product = jnp.dot(rounded, slab_factor.T, preferred_element_type=jnp.float32)
    updated = (slab_rows.astype(jnp.float32) - product).astype(jnp.bfloat16)
    cot_rows = cotangent.reshape(row_count, slab_width)
    factor_grad = -jnp.dot(cot_rows, slab_factor, preferred_element_type=jnp.float32)
    slab_grad = -lax.dot_general(
        cot_rows, rounded, contract_rows, preferred_element_type=jnp.float32
    )
    slab_grad = lax.psum(slab_grad.astype(jnp.bfloat16), "row").astype(jnp.float32)
    grad_tiles = factor_grad.reshape(tiles_local, tile_size, tile_size)
    for column_slot in range(slab_tiles):
        tile_index = column_slot * col_devices + col_index
        is_owner = tile_index % row_devices == row_index
        local_slot = tile_index // row_devices
        current_tile = lax.dynamic_index_in_dim(grad_tiles, local_slot, 0, keepdims=True)
        added_tile = jnp.where(
            is_owner, slab_grad[column_slot * tile_size : (column_slot + 1) * tile_size], 0.0
        )
        grad_tiles = lax.dynamic_update_index_in_dim(
            grad_tiles, current_tile + added_tile[None], local_slot, 0
        )
    factor_grad = grad_tiles.reshape(row_count, tile_size)
    grad_total = lax.psum(factor_grad, "col")
    inverse_strip = lax.dynamic_slice_in_dim(inverse, col_index * strip_width, strip_width, 1)
    grad_panel = jnp.dot(
        grad_total, inverse_strip, precision=highest, preferred_element_type=jnp.float32
    )
    inverse_term = lax.dot_general(
        grad_total, panel_rows, contract_rows, precision=highest, preferred_element_type=jnp.float32
    )
    grad_inverse = lax.psum(inverse_term, "row")
    return (updated.reshape(slab.shape), grad_panel.reshape(panel.shape), grad_inverse)


def solution(mesh):
    in_specs = (
        P(None, "row", None, "col"),
        P(None, "row", None, None, "col", None),
        P(None, "row", None, None, "col", None),
        P(),
    )
    out_specs = (
        P(None, "row", None, None, "col", None),
        P(None, "row", None, "col"),
        P(None, "col"),
    )
    return jax.shard_map(
        per_device, mesh=mesh, in_specs=in_specs, out_specs=out_specs, check_vma=False
    )
```

profile of v0, /device:TPU:6, one launch (start us, length us, event | category | flops | bytes accessed | tf_op | source)
XLA Modules:
  0.0 429.3 jit_solution(7106329265095890)
XLA Ops:
  7.2 1.7 copy.19
  9.1 5.2 %copy.20 = bf16[256,8,4,256]{3,1,2,0:T(8,128)(2,1)} copy(bf16[256,8,4,256]{3,2,1,0:T(4,128)(2,1)} %bitcast.71) | data formatting | bytes 8388608
  14.3 25.3 %all-gather.2.cloned.1.call-done = f32[2048,256]{0,1:T(8,128)} async-done(((f32[2048,32]{0,1:T(8,128)}), f32[2048,256]{0,1:T(8,128)}) %all-gather.2.cloned.1.call-update) | async-done | bytes 2097168 | tf_op jit(solution)/shard_map/all_gather | solution.py:21
  39.6 5.0 %convolution_convert_fusion = bf16[2048,256]{1,0:T(8,128)(2,1)S(1)} fusion(f32[2048,256]{0,1:T(8,128)} %all-gather.2.cloned.1.call-done, f32[256,256]{1,0:T(8,128)S(1)} %copy-done), kind=kOutput, calls=%fused_computation.2 | convolution fusion | flops 1611137024 | bytes 3407872 | tf_op jit(solution)/shard_map/dot_general | solution.py:22
  44.6 4.3 fusion.1
  48.9 0.9 pad_maximum_fusion
  49.8 0.2 all-reduce.4.cloned.1.call-start
  50.0 150.9 %all-reduce.6.cloned.1.call-done = (bf16[1024,256]{1,0:T(8,128)(2,1)}, bf16[1024,256]{0,1:T(8,128)(2,1)}) async-done(((bf16[1024,256]{1,0:T(8,128)(2,1)}, bf16[1024,256]{0,1:T(8,128)(2,1)}), (bf16[1024,256]{1,0:T(8,128)(2,1)}, bf16[1024,256]{0,1:T(8,128)(2,1)})) %all-reduce.6.cloned.1.call-update) | async-done | bytes 1048592 | tf_op jit(solution)/shard_map/psum | solution.py:34
  200.9 3.7 convolution_negate_fusion
  204.6 0.2 copy.24
  204.8 0.9 copy-done.4
  205.7 0.1 convert_element_type.29
  205.8 0.1 fusion.13
  205.9 0.1 fusion.7
  206.0 1.8 copy.14
  207.9 7.0 %copy.18 = f32[256,8,4,256]{3,1,2,0:T(8,128)} copy(bf16[256,8,4,256]{3,2,1,0:T(4,128)(2,1)} %bitcast.70) | data formatting | bytes 12582912
  214.9 6.8 %subtract_convert_fusion = bf16[2048,1024]{1,0:T(8,128)(2,1)} fusion(f32[2048,1024]{1,0:T(8,128)} %bitcast.66, bf16[2048,256]{1,0:T(8,128)(2,1)S(1)} %convolution_convert_fusion, bf16[1024,256]{1,0:T(8,128)(2,1)S(1)} %copy-done.3), kind=kOutput, calls=%fused_computation | convolution fusion | flops 1077936128 | bytes 14155776 | tf_op jit(solution)/shard_map/dot_general | solution.py:36
  221.7 7.9 %reshape.36 = bf16[8,1,256,4,1,256]{5,3,2,0,4,1:T(4,128)(2,1)} reshape(bf16[2048,1024]{1,0:T(8,128)(2,1)} %subtract_convert_fusion) | data formatting | bytes 8388608 | tf_op jit(solution)/shard_map/reshape | solution.py:66
  229.6 44.1 %all-reduce.4.cloned.1.call-done = f32[2048,256]{1,0:T(8,128)} async-done(((f32[2048,256]{1,0:T(8,128)}), f32[2048,256]{1,0:T(8,128)}) %all-reduce.4.cloned.1.call-update) | async-done | bytes 2097168 | tf_op jit(solution)/shard_map/psum | solution.py:57
  273.7 3.8 fusion.14
  277.5 0.1 copy.21
  277.6 0.8 copy.16
  278.4 1.2 fusion.17
  279.6 143.1 %psum.31 = f32[256,32]{0,1:T(8,128)} all-reduce(f32[256,32]{0,1:T(8,128)S(1)} %fusion.17), channel_id=1, replica_groups=mesh['row'=32,'col'=8] {'row'}, use_global_device_ids=true, to_apply=%region_3.4 | all-reduce | flops 8192 | bytes 65536 | tf_op jit(solution)/shard_map/psum | solution.py:65
  (17 shorter events, 0.3 us)
Async XLA Ops:
  7.2 32.4 %copy-start = (f32[256,256]{1,0:T(8,128)S(1)}, f32[256,256]{1,0:T(8,128)}, u32[]{:S(2)}) copy-start(f32[256,256]{1,0:T(8,128)} %param.7) | copy-start | bytes 786436
  7.2 32.4 %all-gather.2.cloned.1.call-start = ((), (), s32[]{:S(2)}) async-start(), calls=%async_computation | async-start | bytes 2359296 | tf_op jit(solution)/shard_map/all_gather | solution.py:21
  9.0 192.0 %all-reduce.6.cloned.1.call-start = ((), (), s32[]{:S(2)}) async-start(), calls=%async_computation.2 | async-start | bytes 2097152 | tf_op jit(solution)/shard_map/psum | solution.py:34
  49.8 223.9 %all-reduce.4.cloned.1.call-start = ((), (), s32[]{:S(2)}) async-start(), calls=%async_computation.1 | async-start | bytes 4194304 | tf_op jit(solution)/shard_map/psum | solution.py:57
  204.6 1.0 copy-start.4
  207.9 7.0 %copy-start.3 = (bf16[1024,256]{1,0:T(8,128)(2,1)S(1)}, bf16[1024,256]{1,0:T(8,128)(2,1)}, u32[]{:S(2)}) copy-start(bf16[1024,256]{1,0:T(8,128)(2,1)} %get-tuple-element.9) | copy-start | bytes 1572868
  229.6 48.8 %copy-start.2 = (f32[4,8,8,256]{3,1,2,0:T(8,128)S(1)}, f32[4,8,8,256]{3,1,2,0:T(8,128)}, u32[]{:S(2)}) copy-start(f32[4,8,8,256]{3,1,2,0:T(8,128)} %copy.19) | copy-start | bytes 786436
  273.7 4.7 %copy-start.1 = (f32[2048,256]{1,0:T(8,128)S(1)}, f32[2048,256]{1,0:T(8,128)}, u32[]{:S(2)}) copy-start(f32[2048,256]{1,0:T(8,128)} %all-reduce.4.cloned.1.call-done) | copy-start | bytes 6291460
Sparse Core Ops, SparseCore 0:
  9.9 29.6 all-gather.1
  49.9 150.9 all-reduce.5
  208.0 65.6 all-reduce.3
where the time goes:
time: 431 us; the launch traced here: 429 us
  waiting for transfers between devices  220 us (51%)
  blocking collectives  143 us (33%)
  local copies, waits for them, and re-layouts  25.6 us (6%)
  matrix products  24.8 us (6%)
  between operations  13.9 us (3%)
    psum x1, waiting for transfers between devices, per_device(): lax.psum(stacked, 'row').astype(jnp.float32).astype(jnp.bfloat16)  151 us
    psum x1, blocking collectives, per_device(): grad_inverse = lax.psum(inverse_term, 'row')  143 us
    psum x1, waiting for transfers between devices, per_device(): grad_total = lax.psum(factor_grad, 'col')  44.1 us
    all_gather x1, waiting for transfers between devices, per_device(): gathered = lax.all_gather(panel_rows, 'col', axis=1, tiled=True)  25.3 us
    unnamed x15, local copies, waits for them, and re-layouts  15.7 us
  transfers between devices with their start and end apart: 3, of which 3 were waited for; matrix products, arithmetic and copies ran while one was open for 6% of the time, Pallas kernels for 0%

commit v1 on v0

v1 whole, which is shorter than its diff:
```python
import jax
import jax.numpy as jnp
from jax import lax
from jax.experimental import pallas as pl
from jax.experimental.pallas import tpu as pltpu
from jax.sharding import PartitionSpec as P

BF = jnp.bfloat16
F32 = jnp.float32
ANY = pl.ANY
MESH = pl.DeviceIdType.MESH


S_A1, S_A2, S_B1, S_B2, S_B3 = 0, 4, 8, 9, 17
S_E1, S_E2, S_E3 = 21, 25, 33
S_D1, S_D2, S_DG = 41, 44, 56
S_GY, S_GZ = 57, 61
N_SEM = 72


def nn(a, b):
    return jnp.dot(a, b, preferred_element_type=F32)


def nt(a, b):
    return lax.dot_general(a, b, (((1,), (1,)), ((), ())), preferred_element_type=F32)


def halves(value):
    high = value.astype(BF)
    return high, (value - high.astype(F32)).astype(BF)


def kernel(
    panel_ref, slab_ref, cot_ref, inv_ref, upd_ref, gp_ref, gi_ref,
    strip, inv, inv_hi, inv_lo, invt_hi, invt_lo, perm, permt,
    graw, gs, sraw, pt, ft, fn, bpt, topt,
    et_own, et_send, e1, e2s, e2r, piece, zpiece, e3, e3s, esum,
    fgt0, gi, mst, d1, cmb, d2, gpo, gd1, gc, gd2, gyr, gzr, gio,
    ssem, rsem, lsem,
):
    row = lax.axis_index("row")
    col = lax.axis_index("col")
    y, z = row // 8, row % 8
    x, core = col // 2, col % 2
    twin = x * 2 + (1 - core)
    is_root = z == col
    mirror = y * 8 + col

    def x_at(d):
        return (x + d) % 4

    def col_at(d):
        return x_at(d) * 2 + core

    def row_y(d):
        return ((y + d) % 4) * 8 + z

    def row_z(d):
        return y * 8 + (z + d) % 8

    def remote(src, dst, send, recv, to_row, to_col):
        return pltpu.make_async_remote_copy(
            src_ref=src, dst_ref=dst, send_sem=ssem.at[send], recv_sem=rsem.at[recv],
            device_id=(to_row, to_col), device_id_type=MESH,
        )

    in_panel = pltpu.make_async_copy(panel_ref, strip, lsem.at[0])
    in_inv = pltpu.make_async_copy(inv_ref, inv, lsem.at[1])
    in_cot = pltpu.make_async_copy(cot_ref, graw, lsem.at[2])
    in_slab = pltpu.make_async_copy(slab_ref, sraw, lsem.at[3])
    in_panel.start()
    in_inv.start()
    in_cot.start()
    in_slab.start()

    barrier = pltpu.get_barrier_semaphore()

    def hello(to_row, to_col):
        pl.semaphore_signal(barrier, inc=1, device_id=(to_row, to_col), device_id_type=MESH)

    hello(row, twin)
    for d in range(1, 4):
        hello(row, col_at(d))
        hello(row_y(d), col)
    for d in range(1, 8):
        hello(row_z(d), col)

    @pl.when(jnp.logical_not(is_root))
    def _():
        hello(mirror, z)

    in_panel.wait()
    for k in range(8):
        pt[k, col] = strip[k].astype(BF)

    pl.semaphore_wait(barrier, 15 - is_root.astype(jnp.int32))

    b1 = remote(pt.at[0, col], bpt.at[col], S_B1, S_B1, mirror, z)
    b1_in = remote(pt.at[0, col], bpt.at[z], S_B1, S_B1, mirror, z)

    @pl.when(jnp.logical_not(is_root))
    def _():
        b1.start()

    @pl.when(is_root)
    def _():
        bpt[z] = pt[0, col]

    a1 = [remote(pt.at[:, col], pt.at[:, col], S_A1 + d, S_A1 + d, row, col_at(d)) for d in range(1, 4)]
    a1.append(remote(pt.at[:, col], pt.at[:, col], S_A1, S_A1, row, twin))
    for copy in a1:
        copy.start()

    in_inv.wait()
    inv_hi[...], inv_lo[...] = halves(inv[...])
    invt_hi[...], invt_lo[...] = halves(inv[...].T)
    r = lax.broadcasted_iota(jnp.int32, (256, 256), 0)
    q = lax.broadcasted_iota(jnp.int32, (256, 256), 1)
    perm[...] = jnp.where(q == (r % 64) * 4 + r // 64, 1.0, 0.0).astype(BF)
    permt[...] = jnp.where(r == (q % 64) * 4 + q // 64, 1.0, 0.0).astype(BF)
    zpiece[...] = jnp.zeros_like(zpiece)
    gi[...] = jnp.zeros_like(gi)

    @pl.when(jnp.logical_not(is_root))
    def _():
        b1_in.wait_recv()

    b2 = [remote(bpt.at[z], bpt.at[z], S_B2 + d, S_B2 + d, row_z(d), col) for d in range(1, 8)]
    for copy in b2:
        copy.start()

    a2 = []
    for d in range(1, 4):
        origin = x_at(4 - d) * 2 + core
        remote(pt.at[:, origin], pt.at[:, origin], S_A1 + d, S_A1 + d, row, col_at(d)).wait_recv()
        copy = remote(pt.at[:, origin], pt.at[:, origin], S_A2 + d, S_A2 + d, row, twin)
        copy.start()
        a2.append(copy)

    in_cot.wait()

    def split_columns(t, carry):
        block = graw[pl.ds(t * 64, 64)].reshape(256, 256)
        moved = nn(perm[...], block).astype(BF)
        for j in range(4):
            gs[j, pl.ds(t * 64, 64), :] = moved[j * 64 : (j + 1) * 64]
        return carry

    lax.fori_loop(0, 16, split_columns, 0)

    for d in range(1, 8):
        origin = (z + 8 - d) % 8
        remote(bpt.at[origin], bpt.at[origin], S_B2 + d, S_B2 + d, row_z(d), col).wait_recv()
    own_top = bpt[...].reshape(256, 256)
    topt[y] = (nn(inv_hi[...], own_top) + nn(inv_lo[...], own_top)).astype(BF)
    b3 = [remote(topt.at[y], topt.at[y], S_B3 + d, S_B3 + d, row_y(d), col) for d in range(1, 4)]
    for copy in b3:
        copy.start()

    remote(pt.at[:, twin], pt.at[:, twin], S_A1, S_A1, row, twin).wait_recv()
    for d in range(1, 4):
        origin = x_at(4 - d) * 2 + (1 - core)
        remote(pt.at[:, origin], pt.at[:, origin], S_A2 + d, S_A2 + d, row, twin).wait_recv()

    def factor_tile(k, carry):
        tile = pt[k].reshape(256, 256)
        value = nn(inv_hi[...], tile) + nn(inv_lo[...], tile)
        ft[k] = value.astype(BF)
        fn[k] = value.T.astype(BF)
        return carry

    lax.fori_loop(0, 8, factor_tile, 0)
    lax.fori_loop(16, 32, split_columns, 0)

    def column_sum(j):
        total = nn(ft[0], gs[j, 0:256, :])
        for k in range(1, 8):
            total += nn(ft[k], gs[j, k * 256 : (k + 1) * 256, :])
        return total

    e1_out = []
    for d in range(1, 4):
        other = (y + d) % 4
        et_send[d] = column_sum(other).astype(BF)
        copy = remote(et_send.at[d], e1.at[d], S_E1 + d, S_E1 + d, row_y(d), col)
        copy.start()
        e1_out.append(copy)
    et_own[...] = column_sum(y)

    for d in range(1, 4):
        origin = (y + 4 - d) % 4
        remote(topt.at[origin], topt.at[origin], S_B3 + d, S_B3 + d, row_y(d), col).wait_recv()

    def gradient_tile(k):
        start = pl.multiple_of(k * 256, 256)
        total = nt(topt[0], gs[0, pl.ds(start, 256), :])
        for j in range(1, 4):
            total += nt(topt[j], gs[j, pl.ds(start, 256), :])
        return -total

    def inverse_term(tile, high, low):
        return (nt(tile, high) + nt(tile, low)).reshape(4, 2, 32, 256)

    def times_inverse(k, high, low):
        value = nn(invt_hi[...], high) + nn(invt_hi[...], low) + nn(invt_lo[...], high)
        mst[k] = value.reshape(4, 2, 32, 256).astype(BF)

    def gradient_step(k, carry):
        high, low = halves(gradient_tile(k))
        gi[...] += inverse_term(pt[k].reshape(256, 256), high, low)
        times_inverse(k, high, low)
        return carry

    lax.fori_loop(1, 8, gradient_step, 0)
    d1_out = [remote(mst.at[pl.ds(1, 7), :, 1 - core], d1.at[pl.ds(1, 7)], S_D1, S_D1, row, twin)]
    d1_out[0].start()
    first = gradient_tile(0)
    fgt0[...] = first
    first_hi, first_lo = halves(first)
    gi[...] += inverse_term(pt[0].reshape(256, 256), first_hi, first_lo)

    for d in range(1, 4):
        remote(et_send.at[d], e1.at[d], S_E1 + d, S_E1 + d, row_y(d), col).wait_recv()
    total = et_own[...]
    for d in range(1, 4):
        total += e1[d].astype(F32)
    et_own[...] = total
    e2s[...] = total.reshape(8, 32, 256).astype(BF)
    e2_out = [
        remote(e2s.at[(z + d) % 8], e2r.at[d], S_E2 + d, S_E2 + d, row_z(d), col) for d in range(1, 8)
    ]
    for copy in e2_out:
        copy.start()

    def update_tile(k):
        start = pl.multiple_of(k * 256, 256)
        products = [nn(fn[k], topt[j]) for j in range(4)]
        for t in range(4):
            rows = pl.ds(pl.multiple_of(start + t * 64, 64), 64)
            old = nn(perm[...], sraw[rows].reshape(256, 256))
            new = jnp.concatenate(
                [old[j * 64 : (j + 1) * 64] - products[j][t * 64 : (t + 1) * 64] for j in range(4)], axis=0
            ).astype(BF)
            sraw[rows] = nn(permt[...], new).astype(BF).reshape(64, 4, 256)
        pltpu.make_async_copy(sraw.at[pl.ds(start, 256)], upd_ref.at[pl.ds(start, 256)], lsem.at[4 + k]).start()

    in_slab.wait()
    for k in range(3):
        update_tile(k)

    for d in range(1, 8):
        remote(e2s.at[(z + d) % 8], e2r.at[d], S_E2 + d, S_E2 + d, row_z(d), col).wait_recv()
    mine = pl.ds(pl.multiple_of(z * 32, 32), 32)
    total = et_own[mine, :]
    for d in range(1, 8):
        total += e2r[d].astype(F32)
    total = -total
    e3s[...] = total.astype(BF)
    away = (col - z + 8) % 8
    e3_out = remote(e3s, e3.at[z], S_E3, S_E3 + away, y * 8 + col, col)

    @pl.when(jnp.logical_not(is_root))
    def _():
        e3_out.start()

    zpiece[mine, :] = total
    piece_hi, piece_lo = halves(zpiece[...])
    gi[...] += inverse_term(bpt[...].reshape(256, 256), piece_hi, piece_lo)
    dg_out = remote(gi.at[:, 1 - core], gd1, S_DG, S_DG, row, twin)
    dg_out.start()

    def join(lo_k, hi_k):
        for other in range(4):
            for k in range(lo_k, hi_k):
                cmb[other, k] = (mst[k, other, core].astype(F32) + d1[k, other].astype(F32)).astype(BF)

    remote(mst.at[pl.ds(1, 7), :, 1 - core], d1.at[pl.ds(1, 7)], S_D1, S_D1, row, twin).wait_recv()
    join(1, 8)
    d2_out = []
    for d in range(1, 4):
        copy = remote(
            cmb.at[x_at(d), pl.ds(1, 7)], d2.at[d, pl.ds(1, 7)], S_D2 + d, S_D2 + d, row, col_at(d)
        )
        copy.start()
        d2_out.append(copy)

    @pl.when(is_root)
    def _():
        esum[z] = e3s[...]
        for d in range(1, 8):
            origin = (z + 8 - d) % 8
            remote(e3s, e3.at[origin], S_E3, S_E3 + d, row_z(d), col).wait_recv()
            esum[origin] = e3[origin]
        fgt0[...] += esum[...].reshape(256, 256).astype(F32)

    first_hi, first_lo = halves(fgt0[...])
    times_inverse(0, first_hi, first_lo)
    d1_out.append(remote(mst.at[0, :, 1 - core], d1.at[0], S_D1 + 1, S_D1 + 1, row, twin))
    d1_out[1].start()

    dg_out.wait_recv()
    gc[...] = gi[:, core] + gd1[...]
    for d in range(1, 4):
        copy = remote(gc.at[x_at(d)], gd2.at[d], S_D2 + 8 + d, S_D2 + 8 + d, row, col_at(d))
        copy.start()
        d2_out.append(copy)

    update_tile(3)

    d1_out[1].wait_recv()
    join(0, 1)
    for d in range(1, 4):
        copy = remote(cmb.at[x_at(d), 0], d2.at[d, 0], S_D2 + 4 + d, S_D2 + 4 + d, row, col_at(d))
        copy.start()
        d2_out.append(copy)

    for d in range(1, 4):
        remote(gc.at[x_at(d)], gd2.at[d], S_D2 + 8 + d, S_D2 + 8 + d, row, col_at(d)).wait_recv()
    gyr[y] = gc[x] + gd2[1] + gd2[2] + gd2[3]
    gy_out = [remote(gyr.at[y], gyr.at[y], S_GY + d, S_GY + d, row_y(d), col) for d in range(1, 4)]
    for copy in gy_out:
        copy.start()

    update_tile(4)
    update_tile(5)

    for d in range(1, 4):
        origin = (y + 4 - d) % 4
        remote(gyr.at[origin], gyr.at[origin], S_GY + d, S_GY + d, row_y(d), col).wait_recv()
    gzr[z] = gyr[0] + gyr[1] + gyr[2] + gyr[3]
    gz_out = [remote(gzr.at[z], gzr.at[z], S_GZ + d, S_GZ + d, row_z(d), col) for d in range(1, 8)]
    for copy in gz_out:
        copy.start()

    update_tile(6)
    update_tile(7)

    def finish(k):
        value = mst[k, x, core].astype(F32) + d1[k, x].astype(F32)
        for d in range(1, 4):
            value += d2[d, k].astype(F32)
        gpo[k] = value

    for d in range(1, 4):
        remote(
            cmb.at[x_at(d), pl.ds(1, 7)], d2.at[d, pl.ds(1, 7)], S_D2 + d, S_D2 + d, row, col_at(d)
        ).wait_recv()
    for k in range(1, 8):
        finish(k)
    for d in range(1, 4):
        remote(cmb.at[x_at(d), 0], d2.at[d, 0], S_D2 + 4 + d, S_D2 + 4 + d, row, col_at(d)).wait_recv()
    finish(0)
    out_gp = pltpu.make_async_copy(gpo, gp_ref, lsem.at[12])
    out_gp.start()

    for d in range(1, 8):
        origin = (z + 8 - d) % 8
        remote(gzr.at[origin], gzr.at[origin], S_GZ + d, S_GZ + d, row_z(d), col).wait_recv()
    total = gzr[0]
    for k in range(1, 8):
        total += gzr[k]
    gio[...] = total
    out_gi = pltpu.make_async_copy(gio, gi_ref, lsem.at[13])
    out_gi.start()

    @pl.when(jnp.logical_not(is_root))
    def _():
        b1.wait_send()
        e3_out.wait_send()

    for copy in a1 + a2 + b2 + b3 + e1_out + e2_out + d1_out + [dg_out] + d2_out + gy_out + gz_out:
        copy.wait_send()
    for k in range(8):
        rows = pl.ds(k * 256, 256)
        pltpu.make_async_copy(sraw.at[rows], upd_ref.at[rows], lsem.at[4 + k]).wait()
    out_gp.wait()
    out_gi.wait()


def per_device(panel, slab, cotangent, inverse):
    strips = jnp.transpose(panel.reshape(8, 256, 32), (0, 2, 1))
    vmem = pltpu.VMEM
    updated, grad_panel, grad_inverse = pl.pallas_call(
        kernel,
        out_shape=(
            jax.ShapeDtypeStruct((2048, 4, 256), BF),
            jax.ShapeDtypeStruct((8, 32, 256), F32),
            jax.ShapeDtypeStruct((32, 256), F32),
        ),
        in_specs=[pl.BlockSpec(memory_space=ANY)] * 4,
        out_specs=[pl.BlockSpec(memory_space=ANY)] * 3,
        scratch_shapes=[
            vmem((8, 32, 256), F32), vmem((256, 256), F32),
            vmem((256, 256), BF), vmem((256, 256), BF), vmem((256, 256), BF), vmem((256, 256), BF),
            vmem((256, 256), BF), vmem((256, 256), BF),
            vmem((2048, 4, 256), BF), vmem((4, 2048, 256), BF), vmem((2048, 4, 256), BF),
            vmem((8, 8, 32, 256), BF), vmem((8, 256, 256), BF), vmem((8, 256, 256), BF),
            vmem((8, 32, 256), BF), vmem((4, 256, 256), BF),
            vmem((256, 256), F32), vmem((4, 256, 256), BF), vmem((4, 256, 256), BF),
            vmem((8, 32, 256), BF), vmem((8, 32, 256), BF),
            vmem((32, 256), F32), vmem((256, 256), F32),
            vmem((8, 32, 256), BF), vmem((32, 256), BF), vmem((8, 32, 256), BF),
            vmem((256, 256), F32), vmem((4, 2, 32, 256), F32),
            vmem((8, 4, 2, 32, 256), BF), vmem((8, 4, 32, 256), BF),
            vmem((4, 8, 32, 256), BF), vmem((4, 8, 32, 256), BF),
            vmem((8, 32, 256), F32),
            vmem((4, 32, 256), F32), vmem((4, 32, 256), F32), vmem((4, 32, 256), F32),
            vmem((4, 32, 256), F32), vmem((8, 32, 256), F32), vmem((32, 256), F32),
            pltpu.SemaphoreType.DMA((N_SEM,)), pltpu.SemaphoreType.DMA((N_SEM,)), pltpu.SemaphoreType.DMA((16,)),
        ],
        compiler_params=pltpu.CompilerParams(
            collective_id=0, has_side_effects=True, vmem_limit_bytes=48 << 20
        ),
    )(strips, slab.reshape(2048, 4, 256), cotangent.reshape(2048, 4, 256), inverse)
    return (
        updated.reshape(slab.shape),
        jnp.transpose(grad_panel, (0, 2, 1)).reshape(panel.shape),
        jnp.transpose(grad_inverse),
    )


def solution(mesh):
    in_specs = (
        P(None, "row", None, "col"),
        P(None, "row", None, None, "col", None),
        P(None, "row", None, None, "col", None),
        P(),
    )
    out_specs = (
        P(None, "row", None, None, "col", None),
        P(None, "row", None, "col"),
        P(None, "col"),
    )
    return jax.shard_map(
        per_device, mesh=mesh, in_specs=in_specs, out_specs=out_specs, check_vma=False
    )
```

time: 431 us -> 68.4 us (0.16)
  waiting for transfers between devices: 220 us -> 0 us
  blocking collectives: 143 us -> 0 us
  Pallas kernels: 0 us -> 61.3 us
  matrix products: 24.8 us -> 0 us
  local copies, waits for them, and re-layouts: 25.6 us -> 5.22 us
  between operations: 13.9 us -> 0.65 us
    psum x2 -> x0, waiting for transfers between devices: 195 us -> none  [the longest x1 151 us: per_device(): lax.psum(stacked, 'row').astype(jnp.float32).astype(jnp.bfloat16)]
    psum x1 -> x0, blocking collectives: 143 us -> none  [per_device(): grad_inverse = lax.psum(inverse_term, 'row')]
    pallas_call x0 -> x1, Pallas kernels: none -> 61.3 us  [per_device(): pl.pallas_call(kernel, out_shape=(jax.ShapeDtypeStruct((2048, 4, 256), BF...]
    all_gather x1 -> x0, waiting for transfers between devices: 25.3 us -> none  [per_device(): gathered = lax.all_gather(panel_rows, 'col', axis=1, tiled=True)]
    dot_general x6 -> x0, matrix products: 24.8 us -> none  [the longest x1 6.83 us: per_device(): jnp.dot(rounded, slab_factor.T, preferred_element_type=jnp.float32)]
    unnamed x15 -> x7, local copies, waits for them, and re-layouts: 15.7 us -> 5.22 us
    reshape x2 -> x0, local copies, waits for them, and re-layouts: 8.05 us -> none  [the longest x1 7.88 us: per_device(): updated.reshape(slab.shape)]
  transfers between devices with their start and end apart: 3 -> 0, of which waited for: 3 -> 0; matrix products, arithmetic and copies ran while one was open for 6% -> 0% of each run, Pallas kernels for 0% -> 0%
where the time goes in v1:
time: 68.4 us; the launch traced here: 67.2 us
  Pallas kernels  61.3 us (90%)
  local copies, waits for them, and re-layouts  5.22 us (8%)
    pallas_call x1, Pallas kernels, per_device(): pl.pallas_call(kernel, out_shape=(jax.ShapeDtypeStruct((2048, 4, 256), BF...  61.3 us
    unnamed x7, local copies, waits for them, and re-layouts  5.22 us

profile of v1, /device:TPU:6, one launch (start us, length us, event | category | flops | bytes accessed | tf_op | source)
XLA Modules:
  0.0 67.2 jit_solution(12861535192341837064)
XLA Ops:
  0.6 0.0 copy-start
  0.6 0.9 %copy-done = f32[8,1,256,32]{2,3,1,0:T(8,128)S(1)} copy-done((f32[8,1,256,32]{2,3,1,0:T(8,128)S(1)}, f32[8,1,256,32]{2,3,1,0:T(8,128)}, u32[]{:S(2)}) %copy-start) | copy-done | bytes 262168
  1.6 0.0 copy-start.1
  1.6 0.9 %copy-done.1 = f32[256,256]{1,0:T(8,128)S(1)} copy-done((f32[256,256]{1,0:T(8,128)S(1)}, f32[256,256]{1,0:T(8,128)}, u32[]{:S(2)}) %copy-start.1) | copy-done | bytes 262168
  2.5 61.3 %shard_map.67 = (bf16[2048,4,256]{2,1,0:T(4,128)(2,1)S(1)}, f32[8,32,256]{2,1,0:T(8,128)S(1)}, f32[32,256]{1,0:T(8,128)S(1)}) custom-call(f32[8,32,256]{2,1,0:T(8,128)S(1)} %bitcast.15, bf16[2048,4,256]{2,1,0:T(4,128)(2,1)} %bitcast.18, bf16[2048,4,256]{2,1,0:T(4,128)(2,1)} %bitcast.19, f32[256,256]{1,0:T(8,128)S(1)} %copy-done.1), custom_call_target="tpu_custom_call" | custom-call | tf_op jit(solution)/shard_map/pallas_call | solution.py:384
  63.9 2.0 %copy.12 = bf16[8,1,256,4,1,256]{5,3,4,2,1,0:T(4,128)(2,1)} copy(bf16[8,1,256,4,1,256]{5,3,4,2,1,0:T(4,128)(2,1)S(1)} %bitcast.14) | data formatting | bytes 8388608
  65.9 0.7 %copy.13 = f32[8,1,256,32]{2,3,1,0:T(8,128)} copy(f32[8,1,256,32]{2,3,1,0:T(8,128)S(1)} %bitcast.16) | data formatting | bytes 524288
  66.6 0.6 copy.14
Async XLA Ops:
  0.6 1.0 %copy-start = (f32[8,1,256,32]{2,3,1,0:T(8,128)S(1)}, f32[8,1,256,32]{2,3,1,0:T(8,128)}, u32[]{:S(2)}) copy-start(f32[8,1,256,32]{2,3,1,0:T(8,128)} %param.4) | copy-start | bytes 786436
  1.6 0.9 %copy-start.1 = (f32[256,256]{1,0:T(8,128)S(1)}, f32[256,256]{1,0:T(8,128)}, u32[]{:S(2)}) copy-start(f32[256,256]{1,0:T(8,128)} %inv_ref.1) | copy-start | bytes 786436

commit v2 on v0

v2 whole, which is shorter than its diff:
```python
import jax
import jax.numpy as jnp
from jax import lax
from jax.experimental import pallas as pl
from jax.experimental.pallas import tpu as pltpu
from jax.sharding import PartitionSpec as P

BF = jnp.bfloat16
F32 = jnp.float32
MESH = pl.DeviceIdType.MESH


S_A1, S_A2, S_B1, S_B2, S_B3 = 0, 8, 16, 17, 25
S_E1, S_E2, S_E3 = 29, 37, 45
S_D1, S_D2, S_WC, S_WX, S_WY, S_WZ = 46, 48, 56, 57, 61, 65
N_SEM = 73


def nn(a, b):
    return jnp.dot(a, b, preferred_element_type=F32)


def nt(a, b):
    return lax.dot_general(a, b, (((1,), (1,)), ((), ())), preferred_element_type=F32)


def halves(value):
    high = value.astype(BF)
    return high, (value - high.astype(F32)).astype(BF)


def three(high, low, other_high, other_low, product):
    return product(high, other_high) + product(high, other_low) + product(low, other_high)


def kernel(
    panel_ref, slab_ref, cot_ref, inv_ref, upd_ref, gp_ref, gi_ref,
    strip, inv, inv_hi, inv_lo, k_hi, k_lo, perm, permt,
    graw, gs, sraw, pt, fn, tp, topt,
    q_sum, n_own, n_send, e1, e2s, e2r, e3s, e3,
    r_hi, r_lo, w, mst, d1, cmb, d2, wd, wc, wx, wy, wz,
    ssem, rsem, lsem,
):
    row = lax.axis_index("row")
    col = lax.axis_index("col")
    y, z = row // 8, row % 8
    x, core = col // 2, col % 2
    twin = x * 2 + (1 - core)
    is_root = z == col
    mirror = y * 8 + col

    def x_at(d):
        return (x + d) % 4

    def col_at(d):
        return x_at(d) * 2 + core

    def row_y(d):
        return ((y + d) % 4) * 8 + z

    def row_z(d):
        return y * 8 + (z + d) % 8

    def remote(src, dst, send, recv, to_row, to_col):
        return pltpu.make_async_remote_copy(
            src_ref=src, dst_ref=dst, send_sem=ssem.at[send], recv_sem=rsem.at[recv],
            device_id=(to_row, to_col), device_id_type=MESH,
        )

    sent = []

    def send(src, dst, sem, to_row, to_col):
        copy = remote(src, dst, sem, sem, to_row, to_col)
        copy.start()
        sent.append(copy)

    def arrived(dst, sem):
        remote(dst, dst, sem, sem, row, twin).wait_recv()

    in_panel = pltpu.make_async_copy(panel_ref, strip, lsem.at[0])
    in_inv = pltpu.make_async_copy(inv_ref, inv, lsem.at[1])
    in_cot = pltpu.make_async_copy(cot_ref, graw, lsem.at[2])
    in_slab = pltpu.make_async_copy(slab_ref, sraw, lsem.at[3])
    in_panel.start()
    in_inv.start()
    in_cot.start()

    barrier = pltpu.get_barrier_semaphore()

    def hello(to_row, to_col):
        pl.semaphore_signal(barrier, inc=1, device_id=(to_row, to_col), device_id_type=MESH)

    hello(row, twin)
    for d in range(1, 4):
        hello(row, col_at(d))
        hello(row_y(d), col)
    for d in range(1, 8):
        hello(row_z(d), col)

    @pl.when(jnp.logical_not(is_root))
    def _():
        hello(mirror, z)

    in_panel.wait()
    for k in range(8):
        pt[k, col] = strip[k].astype(BF)

    pl.semaphore_wait(barrier, 15 - is_root.astype(jnp.int32))

    b1 = remote(pt.at[0, col], tp.at[y, col], S_B1, S_B1, mirror, z)

    @pl.when(jnp.logical_not(is_root))
    def _():
        b1.start()

    @pl.when(is_root)
    def _():
        tp[y, z] = pt[0, col]

    def half(h, c):
        return pt.at[pl.ds(4 * h, 4), c]

    for h in range(2):
        for d in (1, 3, 2):
            send(half(h, col), half(h, col), S_A1 + 4 * h + d, row, col_at(d))
        send(half(h, col), half(h, col), S_A1 + 4 * h, row, twin)
    in_slab.start()

    def pass_on(h, d):
        origin = x_at(4 - d) * 2 + core
        arrived(half(h, origin), S_A1 + 4 * h + d)
        send(half(h, origin), half(h, origin), S_A2 + 4 * h + d, row, twin)

    def to_other_y(piece):
        for d in range(1, 4):
            remote(tp.at[y, piece], tp.at[y, piece], S_B3 + d, S_B3 + d, row_y(d), col).start()

    def piece_from(d):
        origin = (z + 8 - d) % 8
        arrived(tp.at[y, origin], S_B2 + d)
        to_other_y(origin)

    r = lax.broadcasted_iota(jnp.int32, (256, 256), 0)
    q = lax.broadcasted_iota(jnp.int32, (256, 256), 1)
    perm[...] = jnp.where(q == (r % 64) * 4 + r // 64, 1.0, 0.0).astype(BF)
    permt[...] = jnp.where(r == (q % 64) * 4 + q // 64, 1.0, 0.0).astype(BF)

    in_cot.wait()

    def split_columns(t, carry):
        block = graw[pl.ds(t * 64, 64)].reshape(256, 256)
        moved = nn(perm[...], block).astype(BF)
        for j in range(4):
            gs[j, pl.ds(t * 64, 64), :] = moved[j * 64 : (j + 1) * 64]
        return carry

    @pl.when(jnp.logical_not(is_root))
    def _():
        arrived(tp.at[y, z], S_B1)

    for d in (4, 3, 5, 2, 6, 1, 7):
        send(tp.at[y, z], tp.at[y, z], S_B2 + d, row_z(d), col)
    to_other_y(z)

    lax.fori_loop(0, 4, split_columns, 0)
    pass_on(0, 1)
    pass_on(0, 3)
    piece_from(1)
    piece_from(7)
    lax.fori_loop(4, 8, split_columns, 0)
    pass_on(0, 2)
    piece_from(2)
    piece_from(6)
    lax.fori_loop(8, 14, split_columns, 0)
    pass_on(1, 1)
    pass_on(1, 3)
    piece_from(3)
    piece_from(5)
    lax.fori_loop(14, 18, split_columns, 0)
    piece_from(4)
    pass_on(1, 2)
    lax.fori_loop(18, 32, split_columns, 0)

    in_inv.wait()
    high, low = halves(inv[...])
    inv_hi[...], inv_lo[...] = high, low
    t_high, t_low = halves(inv[...].T)
    k_hi[...], k_lo[...] = halves(three(t_high, t_low, high, low, nn))

    def panel_half(h):
        arrived(half(h, twin), S_A1 + 4 * h)
        for d in range(1, 4):
            origin = x_at(4 - d) * 2 + (1 - core)
            arrived(half(h, origin), S_A2 + 4 * h + d)

    def row_sum(j, h):
        total = nn(pt[4 * h].reshape(256, 256), gs[j, pl.ds(4 * h * 256, 256), :])
        for k in range(4 * h + 1, 4 * h + 4):
            total += nn(pt[k].reshape(256, 256), gs[j, pl.ds(k * 256, 256), :])
        return total

    def first_rows(j, carry):
        q_sum[j] = row_sum(j, 0)
        return carry

    panel_half(0)
    lax.fori_loop(0, 4, first_rows, 0)
    panel_half(1)

    def times_k(value):
        high, low = halves(value)
        return three(k_hi[...], k_lo[...], high, low, nn)

    for d in (2, 1, 3):
        other = (y + d) % 4
        total = q_sum[other] + row_sum(other, 1)
        q_sum[other] = total
        n_send[d] = times_k(total).astype(BF)
        for h in range(2):
            rows = pl.ds(128 * h, 128)
            send(n_send.at[d, rows], e1.at[d, rows], S_E1 + 4 * h + d, row_y(d), col)
    total = q_sum[y] + row_sum(y, 1)
    q_sum[y] = total
    n_own[...] = times_k(total)

    for d in range(1, 4):
        arrived(tp.at[(y + 4 - d) % 4], S_B3 + d)

    def column_sum(t, carry):
        rows = pl.ds(pl.multiple_of(t * 256, 256), 256)
        total = nt(gs[0, rows, :], tp[0].reshape(256, 256))
        for j in range(1, 4):
            total += nt(gs[j, rows, :], tp[j].reshape(256, 256))
        high, low = halves(total)
        r_hi[rows, :] = high
        r_lo[rows, :] = low
        tile = pt[t].reshape(256, 256)
        w[...] += (nn(tile, high) + nn(tile, low)).reshape(4, 2, 32, 256)
        return carry

    total = jnp.zeros((256, 256), F32)
    for j in range(4):
        high, low = halves(q_sum[j])
        tile = tp[j].reshape(256, 256)
        total += nt(tile, high) + nt(tile, low)
    w[...] = total.reshape(4, 2, 32, 256)
    lax.fori_loop(0, 8, column_sum, 0)
    send(w.at[:, 1 - core], wd, S_WC, row, twin)

    def k_tile(k, carry):
        rows = pl.ds(pl.multiple_of(k * 256, 256), 256)
        value = three(k_hi[...], k_lo[...], r_hi[rows, :], r_lo[rows, :], nt)
        mst[k] = value.reshape(4, 2, 32, 256).astype(BF)
        return carry

    def core_half(h):
        send(mst.at[pl.ds(4 * h, 4), :, 1 - core], d1.at[pl.ds(4 * h, 4)], S_D1 + h, row, twin)

    def join(h):
        arrived(d1.at[pl.ds(4 * h, 4)], S_D1 + h)
        for other in range(4):
            for k in range(4 * h, 4 * h + 4):
                cmb[other, k] = (mst[k, other, core].astype(F32) + d1[k, other].astype(F32)).astype(BF)
        for d in (1, 3, 2):
            part = pl.ds(4 * h, 4)
            send(cmb.at[x_at(d), part], d2.at[d, part], S_D2 + 4 * h + d, row, col_at(d))

    def strips_out(h):
        rows = pl.ds(128 * h, 128)
        total = n_own[rows, :]
        for d in range(1, 4):
            arrived(e1.at[d, rows], S_E1 + 4 * h + d)
            total += e1[d, rows, :].astype(F32)
        n_own[rows, :] = total
        e2s[pl.ds(4 * h, 4)] = total.reshape(4, 32, 256).astype(BF)
        for other in range(4 * h, 4 * h + 4):

            @pl.when(z != other)
            def _():
                remote(e2s.at[other], e2r.at[z], S_E2 + other, S_E2 + z, y * 8 + other, col).start()

    lax.fori_loop(0, 4, k_tile, 0)
    core_half(0)

    arrived(wd, S_WC)
    wc[...] = w[:, core] + wd[...]
    for d in (2, 1, 3):
        send(wc.at[x_at(d)], wx.at[d], S_WX + d, row, col_at(d))

    lax.fori_loop(4, 8, k_tile, 0)
    core_half(1)
    join(0)
    strips_out(0)
    join(1)
    strips_out(1)

    for d in range(1, 4):
        arrived(wx.at[d], S_WX + d)
    total = (wc[x] + wx[1] + wx[2] + wx[3]).astype(BF)
    wy[y] = total
    for d in (2, 1, 3):
        send(wy.at[y], wy.at[y], S_WY + d, row_y(d), col)

    def top_tile(j, carry):
        tile = tp[j].reshape(256, 256)
        topt[j] = (nn(inv_hi[...], tile) + nn(inv_lo[...], tile)).astype(BF)
        return carry

    def factor_tile(k, carry):
        tile = pt[k].reshape(256, 256)
        fn[k] = (nn(inv_hi[...], tile) + nn(inv_lo[...], tile)).T.astype(BF)
        return carry

    lax.fori_loop(0, 4, top_tile, 0)
    lax.fori_loop(0, 4, factor_tile, 0)

    for d in range(1, 4):
        arrived(wy.at[(y + 4 - d) % 4], S_WY + d)
    total = wy[0].astype(F32)
    for k in range(1, 4):
        total += wy[k].astype(F32)
    wz[z] = total.astype(BF)
    for d in (4, 3, 5, 2, 6, 1, 7):
        send(wz.at[z], wz.at[z], S_WZ + d, row_z(d), col)

    for d in range(1, 8):
        origin = (z + 8 - d) % 8
        arrived(e2r.at[origin], S_E2 + origin)
    e2r[z] = jnp.zeros((32, 256), BF)
    total = n_own[pl.ds(pl.multiple_of(z * 32, 32), 32), :]
    for k in range(8):
        total += e2r[k].astype(F32)
    e3s[...] = total.astype(BF)
    e3_out = remote(e3s, e3, S_E3, S_E3, mirror, z)

    @pl.when(jnp.logical_not(is_root))
    def _():
        e3_out.start()

    lax.fori_loop(4, 8, factor_tile, 0)
    in_slab.wait()

    def update_tile(k, carry):
        start = pl.multiple_of(k * 256, 256)
        products = [nn(fn[k], topt[j]) for j in range(4)]
        for t in range(4):
            rows = pl.ds(pl.multiple_of(start + t * 64, 64), 64)
            old = nn(perm[...], sraw[rows].reshape(256, 256))
            new = jnp.concatenate(
                [old[j * 64 : (j + 1) * 64] - products[j][t * 64 : (t + 1) * 64] for j in range(4)], axis=0
            ).astype(BF)
            upd_ref[rows] = nn(permt[...], new).astype(BF).reshape(64, 4, 256)
        return carry

    lax.fori_loop(0, 8, update_tile, 0)

    for h in range(2):
        for d in range(1, 4):
            arrived(d2.at[d, pl.ds(4 * h, 4)], S_D2 + 4 * h + d)
    for k in range(1, 8):
        value = mst[k, x, core].astype(F32) + d1[k, x].astype(F32)
        for d in range(1, 4):
            value += d2[d, k].astype(F32)
        gp_ref[k] = -value

    @pl.when(is_root)
    def _():
        e3[...] = e3s[...]

    @pl.when(jnp.logical_not(is_root))
    def _():
        arrived(e3, S_E3)

    value = mst[0, x, core].astype(F32) + d1[0, x].astype(F32) + e3[...].astype(F32)
    for d in range(1, 4):
        value += d2[d, 0].astype(F32)
    gp_ref[0] = -value

    for d in range(1, 8):
        arrived(wz.at[(z + 8 - d) % 8], S_WZ + d)
    total = wz[0].astype(F32)
    for k in range(1, 8):
        total += wz[k].astype(F32)
    high, low = halves(total)
    gi_ref[...] = -three(high, low, inv_hi[...], inv_lo[...], nt)

    @pl.when(jnp.logical_not(is_root))
    def _():
        b1.wait_send()
        e3_out.wait_send()

    for d in range(1, 4):
        remote(tp.at[y], tp.at[y], S_B3 + d, S_B3 + d, row_y(d), col).wait_send()
    for other in range(8):

        @pl.when(z != other)
        def _():
            remote(e2s.at[other], e2r.at[z], S_E2 + other, S_E2 + z, y * 8 + other, col).wait_send()

    for copy in sent:
        copy.wait_send()


def per_device(panel, slab, cotangent, inverse):
    strips = jnp.transpose(panel.reshape(8, 256, 32), (0, 2, 1))
    vmem = pltpu.VMEM
    updated, grad_panel, grad_inverse = pl.pallas_call(
        kernel,
        out_shape=(
            jax.ShapeDtypeStruct((2048, 4, 256), BF),
            jax.ShapeDtypeStruct((8, 32, 256), F32),
            jax.ShapeDtypeStruct((32, 256), F32),
        ),
        in_specs=[pl.BlockSpec(memory_space=pltpu.HBM)] * 4,
        out_specs=[pl.BlockSpec(memory_space=vmem)] * 3,
        scratch_shapes=[
            vmem((8, 32, 256), F32), vmem((256, 256), F32),
            vmem((256, 256), BF), vmem((256, 256), BF), vmem((256, 256), BF), vmem((256, 256), BF),
            vmem((256, 256), BF), vmem((256, 256), BF),
            vmem((2048, 4, 256), BF), vmem((4, 2048, 256), BF), vmem((2048, 4, 256), BF),
            vmem((8, 8, 32, 256), BF), vmem((8, 256, 256), BF),
            vmem((4, 8, 32, 256), BF), vmem((4, 256, 256), BF),
            vmem((4, 256, 256), F32), vmem((256, 256), F32),
            vmem((4, 256, 256), BF), vmem((4, 256, 256), BF),
            vmem((8, 32, 256), BF), vmem((8, 32, 256), BF),
            vmem((32, 256), BF), vmem((32, 256), BF),
            vmem((2048, 256), BF), vmem((2048, 256), BF), vmem((4, 2, 32, 256), F32),
            vmem((8, 4, 2, 32, 256), BF), vmem((8, 4, 32, 256), BF),
            vmem((4, 8, 32, 256), BF), vmem((4, 8, 32, 256), BF),
            vmem((4, 32, 256), F32), vmem((4, 32, 256), F32), vmem((4, 32, 256), F32),
            vmem((4, 32, 256), BF), vmem((8, 32, 256), BF),
            pltpu.SemaphoreType.DMA((N_SEM,)), pltpu.SemaphoreType.DMA((N_SEM,)), pltpu.SemaphoreType.DMA((4,)),
        ],
        compiler_params=pltpu.CompilerParams(
            collective_id=0, has_side_effects=True, vmem_limit_bytes=48 << 20
        ),
    )(strips, slab.reshape(2048, 4, 256), cotangent.reshape(2048, 4, 256), inverse)
    return (
        updated.reshape(slab.shape),
        jnp.transpose(grad_panel, (0, 2, 1)).reshape(panel.shape),
        jnp.transpose(grad_inverse),
    )


def solution(mesh):
    in_specs = (
        P(None, "row", None, "col"),
        P(None, "row", None, None, "col", None),
        P(None, "row", None, None, "col", None),
        P(),
    )
    out_specs = (
        P(None, "row", None, None, "col", None),
        P(None, "row", None, "col"),
        P(None, "col"),
    )
    return jax.shard_map(
        per_device, mesh=mesh, in_specs=in_specs, out_specs=out_specs, check_vma=False
    )
```

time: 431 us -> 59.2 us (0.14)
  waiting for transfers between devices: 220 us -> 0 us
  blocking collectives: 143 us -> 0 us
  Pallas kernels: 0 us -> 52.7 us
  matrix products: 24.8 us -> 0 us
  local copies, waits for them, and re-layouts: 25.6 us -> 5.22 us
  between operations: 13.9 us -> 0.65 us
    psum x2 -> x0, waiting for transfers between devices: 195 us -> none  [the longest x1 151 us: per_device(): lax.psum(stacked, 'row').astype(jnp.float32).astype(jnp.bfloat16)]
    psum x1 -> x0, blocking collectives: 143 us -> none  [per_device(): grad_inverse = lax.psum(inverse_term, 'row')]
    pallas_call x0 -> x1, Pallas kernels: none -> 52.7 us  [per_device(): pl.pallas_call(kernel, out_shape=(jax.ShapeDtypeStruct((2048, 4, 256), BF...]
    all_gather x1 -> x0, waiting for transfers between devices: 25.3 us -> none  [per_device(): gathered = lax.all_gather(panel_rows, 'col', axis=1, tiled=True)]
    dot_general x6 -> x0, matrix products: 24.8 us -> none  [the longest x1 6.83 us: per_device(): jnp.dot(rounded, slab_factor.T, preferred_element_type=jnp.float32)]
    unnamed x15 -> x7, local copies, waits for them, and re-layouts: 15.7 us -> 5.22 us
    reshape x2 -> x0, local copies, waits for them, and re-layouts: 8.05 us -> none  [the longest x1 7.88 us: per_device(): updated.reshape(slab.shape)]
  transfers between devices with their start and end apart: 3 -> 0, of which waited for: 3 -> 0; matrix products, arithmetic and copies ran while one was open for 6% -> 0% of each run, Pallas kernels for 0% -> 0%
where the time goes in v2:
time: 59.2 us; the launch traced here: 58.6 us
  Pallas kernels  52.7 us (89%)
  local copies, waits for them, and re-layouts  5.22 us (9%)
  between operations  0.65 us (1%)
    pallas_call x1, Pallas kernels, per_device(): pl.pallas_call(kernel, out_shape=(jax.ShapeDtypeStruct((2048, 4, 256), BF...  52.7 us
    unnamed x7, local copies, waits for them, and re-layouts  5.22 us

profile of v2, /device:TPU:6, one launch (start us, length us, event | category | flops | bytes accessed | tf_op | source)
XLA Modules:
  0.0 58.6 jit_solution(2691419418927957360)
XLA Ops:
  0.6 0.0 copy-start
  0.6 0.9 %copy-done = f32[8,1,256,32]{2,3,1,0:T(8,128)S(1)} copy-done((f32[8,1,256,32]{2,3,1,0:T(8,128)S(1)}, f32[8,1,256,32]{2,3,1,0:T(8,128)}, u32[]{:S(2)}) %copy-start) | copy-done | bytes 262168
  1.6 0.0 copy-start.1
  1.6 0.9 %copy-done.1 = f32[256,256]{1,0:T(8,128)S(1)} copy-done((f32[256,256]{1,0:T(8,128)S(1)}, f32[256,256]{1,0:T(8,128)}, u32[]{:S(2)}) %copy-start.1) | copy-done | bytes 262168
  2.5 52.7 %shard_map.67 = (bf16[2048,4,256]{2,1,0:T(4,128)(2,1)S(1)}, f32[8,32,256]{2,1,0:T(8,128)S(1)}, f32[32,256]{1,0:T(8,128)S(1)}) custom-call(f32[8,32,256]{2,1,0:T(8,128)S(1)} %bitcast.15, bf16[2048,4,256]{2,1,0:T(4,128)(2,1)} %bitcast.18, bf16[2048,4,256]{2,1,0:T(4,128)(2,1)} %bitcast.19, f32[256,256]{1,0:T(8,128)S(1)} %copy-done.1), custom_call_target="tpu_custom_call" | custom-call | tf_op jit(solution)/shard_map/pallas_call | solution.py:407
  55.2 2.0 %copy.12 = bf16[8,1,256,4,1,256]{5,3,4,2,1,0:T(4,128)(2,1)} copy(bf16[8,1,256,4,1,256]{5,3,4,2,1,0:T(4,128)(2,1)S(1)} %bitcast.14) | data formatting | bytes 8388608
  57.3 0.7 %copy.13 = f32[8,1,256,32]{2,3,1,0:T(8,128)} copy(f32[8,1,256,32]{2,3,1,0:T(8,128)S(1)} %bitcast.16) | data formatting | bytes 524288
  58.0 0.6 %copy.14 = f32[256,32]{0,1:T(8,128)} copy(f32[256,32]{0,1:T(8,128)S(1)} %bitcast.17) | data formatting | bytes 65536
Async XLA Ops:
  0.6 1.0 %copy-start = (f32[8,1,256,32]{2,3,1,0:T(8,128)S(1)}, f32[8,1,256,32]{2,3,1,0:T(8,128)}, u32[]{:S(2)}) copy-start(f32[8,1,256,32]{2,3,1,0:T(8,128)} %param.4) | copy-start | bytes 786436
  1.6 0.9 %copy-start.1 = (f32[256,256]{1,0:T(8,128)S(1)}, f32[256,256]{1,0:T(8,128)}, u32[]{:S(2)}) copy-start(f32[256,256]{1,0:T(8,128)} %inv_ref.1) | copy-start | bytes 786436

commit v3 on v2

--- a/solution.py
+++ b/solution.py
@@ -37,8 +37,8 @@
     panel_ref, slab_ref, cot_ref, inv_ref, upd_ref, gp_ref, gi_ref,
     strip, inv, inv_hi, inv_lo, k_hi, k_lo, perm, permt,
     graw, gs, sraw, pt, fn, tp, topt,
-    q_sum, n_own, n_send, e1, e2s, e2r, e3s, e3,
-    r_hi, r_lo, w, mst, d1, cmb, d2, wd, wc, wx, wy, wz,
+    q_sum, q_bf, n_own, n_send, e1, e2s, e2r, e3s, e3,
+    r_bf, w, mst, d1, cmb, d2, wd, wc, wx, wy, wz, gpo, gio,
     ssem, rsem, lsem,
 ):
     row = lax.axis_index("row")
@@ -105,6 +105,16 @@
     for k in range(8):
         pt[k, col] = strip[k].astype(BF)
 
+    r = lax.broadcasted_iota(jnp.int32, (256, 256), 0)
+    q = lax.broadcasted_iota(jnp.int32, (256, 256), 1)
+    perm[...] = jnp.where(q == (r % 64) * 4 + r // 64, 1.0, 0.0).astype(BF)
+    permt[...] = jnp.where(r == (q % 64) * 4 + q // 64, 1.0, 0.0).astype(BF)
+    in_inv.wait()
+    high, low = halves(inv[...])
+    inv_hi[...], inv_lo[...] = high, low
+    t_high, t_low = halves(inv[...].T)
+    k_hi[...], k_lo[...] = halves(three(t_high, t_low, high, low, nn))
+
     pl.semaphore_wait(barrier, 15 - is_root.astype(jnp.int32))
 
     b1 = remote(pt.at[0, col], tp.at[y, col], S_B1, S_B1, mirror, z)
@@ -140,18 +150,13 @@
         arrived(tp.at[y, origin], S_B2 + d)
         to_other_y(origin)
 
-    r = lax.broadcasted_iota(jnp.int32, (256, 256), 0)
-    q = lax.broadcasted_iota(jnp.int32, (256, 256), 1)
-    perm[...] = jnp.where(q == (r % 64) * 4 + r // 64, 1.0, 0.0).astype(BF)
-    permt[...] = jnp.where(r == (q % 64) * 4 + q // 64, 1.0, 0.0).astype(BF)
-
     in_cot.wait()
 
     def split_columns(t, carry):
         block = graw[pl.ds(t * 64, 64)].reshape(256, 256)
         moved = nn(perm[...], block).astype(BF)
         for j in range(4):
-            gs[j, pl.ds(t * 64, 64), :] = moved[j * 64 : (j + 1) * 64]
+            gs[pl.ds(t * 64, 64), j * 256 : (j + 1) * 256] = moved[j * 64 : (j + 1) * 64]
         return carry
 
     @pl.when(jnp.logical_not(is_root))
@@ -162,30 +167,24 @@
         send(tp.at[y, z], tp.at[y, z], S_B2 + d, row_z(d), col)
     to_other_y(z)
 
-    lax.fori_loop(0, 4, split_columns, 0)
+    lax.fori_loop(0, 4, split_columns, 0, unroll=2)
     pass_on(0, 1)
     pass_on(0, 3)
     piece_from(1)
     piece_from(7)
-    lax.fori_loop(4, 8, split_columns, 0)
+    lax.fori_loop(4, 8, split_columns, 0, unroll=2)
     pass_on(0, 2)
     piece_from(2)
     piece_from(6)
-    lax.fori_loop(8, 14, split_columns, 0)
+    lax.fori_loop(8, 14, split_columns, 0, unroll=2)
     pass_on(1, 1)
     pass_on(1, 3)
     piece_from(3)
     piece_from(5)
-    lax.fori_loop(14, 18, split_columns, 0)
+    lax.fori_loop(14, 18, split_columns, 0, unroll=2)
     piece_from(4)
     pass_on(1, 2)
-    lax.fori_loop(18, 32, split_columns, 0)
-
-    in_inv.wait()
-    high, low = halves(inv[...])
-    inv_hi[...], inv_lo[...] = high, low
-    t_high, t_low = halves(inv[...].T)
-    k_hi[...], k_lo[...] = halves(three(t_high, t_low, high, low, nn))
+    lax.fori_loop(18, 32, split_columns, 0, unroll=2)
 
     def panel_half(h):
         arrived(half(h, twin), S_A1 + 4 * h)
@@ -193,63 +192,45 @@
             origin = x_at(4 - d) * 2 + (1 - core)
             arrived(half(h, origin), S_A2 + 4 * h + d)
 
-    def row_sum(j, h):
-        total = nn(pt[4 * h].reshape(256, 256), gs[j, pl.ds(4 * h * 256, 256), :])
-        for k in range(4 * h + 1, 4 * h + 4):
-            total += nn(pt[k].reshape(256, 256), gs[j, pl.ds(k * 256, 256), :])
-        return total
-
-    def first_rows(j, carry):
-        q_sum[j] = row_sum(j, 0)
-        return carry
+    def panel_rows(k0, k1):
+        return jnp.concatenate([pt[k].reshape(256, 256) for k in range(k0, k1)], axis=1)
 
     panel_half(0)
-    lax.fori_loop(0, 4, first_rows, 0)
+    q_sum[...] = nn(panel_rows(0, 4), gs[0:1024, :])
     panel_half(1)
 
-    def times_k(value):
-        high, low = halves(value)
-        return three(k_hi[...], k_lo[...], high, low, nn)
+    def column_tile(j):
+        columns = pl.ds(pl.multiple_of(j * 256, 256), 256)
+        total = (q_sum[:, columns] + nn(panel_rows(4, 8), gs[1024:2048, columns])).astype(BF)
+        q_bf[j] = total
+        return nn(k_hi[...], total) + nn(k_lo[...], total)
 
     for d in (2, 1, 3):
-        other = (y + d) % 4
-        total = q_sum[other] + row_sum(other, 1)
-        q_sum[other] = total
-        n_send[d] = times_k(total).astype(BF)
+        n_send[d] = column_tile((y + d) % 4).astype(BF)
         for h in range(2):
             rows = pl.ds(128 * h, 128)
             send(n_send.at[d, rows], e1.at[d, rows], S_E1 + 4 * h + d, row_y(d), col)
-    total = q_sum[y] + row_sum(y, 1)
-    q_sum[y] = total
-    n_own[...] = times_k(total)
+    n_own[...] = column_tile(y)
 
     for d in range(1, 4):
         arrived(tp.at[(y + 4 - d) % 4], S_B3 + d)
 
+    def top_columns():
+        return jnp.concatenate([tp[j].reshape(256, 256) for j in range(4)], axis=1)
+
     def column_sum(t, carry):
-        rows = pl.ds(pl.multiple_of(t * 256, 256), 256)
-        total = nt(gs[0, rows, :], tp[0].reshape(256, 256))
-        for j in range(1, 4):
-            total += nt(gs[j, rows, :], tp[j].reshape(256, 256))
-        high, low = halves(total)
-        r_hi[rows, :] = high
-        r_lo[rows, :] = low
-        tile = pt[t].reshape(256, 256)
-        w[...] += (nn(tile, high) + nn(tile, low)).reshape(4, 2, 32, 256)
-        return carry
-
-    total = jnp.zeros((256, 256), F32)
-    for j in range(4):
-        high, low = halves(q_sum[j])
-        tile = tp[j].reshape(256, 256)
-        total += nt(tile, high) + nt(tile, low)
-    w[...] = total.reshape(4, 2, 32, 256)
-    lax.fori_loop(0, 8, column_sum, 0)
+        rows = pl.ds(pl.multiple_of(t * 512, 512), 512)
+        r_bf[rows, :] = nt(gs[rows, :], top_columns()).astype(BF)
+        return carry
+
+    lax.fori_loop(0, 4, column_sum, 0)
+    q_all = jnp.concatenate([q_bf[j] for j in range(4)], axis=1)
+    w[...] = (nn(panel_rows(0, 8), r_bf[...]) + nt(top_columns(), q_all)).reshape(4, 2, 32, 256)
     send(w.at[:, 1 - core], wd, S_WC, row, twin)
 
     def k_tile(k, carry):
         rows = pl.ds(pl.multiple_of(k * 256, 256), 256)
-        value = three(k_hi[...], k_lo[...], r_hi[rows, :], r_lo[rows, :], nt)
+        value = nt(k_hi[...], r_bf[rows, :]) + nt(k_lo[...], r_bf[rows, :])
         mst[k] = value.reshape(4, 2, 32, 256).astype(BF)
         return carry
 
@@ -340,16 +321,19 @@
     lax.fori_loop(4, 8, factor_tile, 0)
     in_slab.wait()
 
+    def out_rows(k):
+        rows = pl.ds(pl.multiple_of(k * 256, 256), 256)
+        return pltpu.make_async_copy(sraw.at[rows], upd_ref.at[rows], lsem.at[4 + k])
+
     def update_tile(k, carry):
         start = pl.multiple_of(k * 256, 256)
-        products = [nn(fn[k], topt[j]) for j in range(4)]
+        products = [nn(fn[k], topt[j]).astype(BF) for j in range(4)]
         for t in range(4):
             rows = pl.ds(pl.multiple_of(start + t * 64, 64), 64)
-            old = nn(perm[...], sraw[rows].reshape(256, 256))
-            new = jnp.concatenate(
-                [old[j * 64 : (j + 1) * 64] - products[j][t * 64 : (t + 1) * 64] for j in range(4)], axis=0
-            ).astype(BF)
-            upd_ref[rows] = nn(permt[...], new).astype(BF).reshape(64, 4, 256)
+            product = jnp.concatenate([products[j][t * 64 : (t + 1) * 64] for j in range(4)], axis=0)
+            old = sraw[rows].reshape(256, 256).astype(F32)
+            sraw[rows] = (old - nn(permt[...], product)).astype(BF).reshape(64, 4, 256)
+        out_rows(k).start()
         return carry
 
     lax.fori_loop(0, 8, update_tile, 0)
@@ -361,7 +345,7 @@
         value = mst[k, x, core].astype(F32) + d1[k, x].astype(F32)
         for d in range(1, 4):
             value += d2[d, k].astype(F32)
-        gp_ref[k] = -value
+        gpo[k] = -value
 
     @pl.when(is_root)
     def _():
@@ -374,7 +358,9 @@
     value = mst[0, x, core].astype(F32) + d1[0, x].astype(F32) + e3[...].astype(F32)
     for d in range(1, 4):
         value += d2[d, 0].astype(F32)
-    gp_ref[0] = -value
+    gpo[0] = -value
+    out_gp = pltpu.make_async_copy(gpo, gp_ref, lsem.at[12])
+    out_gp.start()
 
     for d in range(1, 8):
         arrived(wz.at[(z + 8 - d) % 8], S_WZ + d)
@@ -382,7 +368,9 @@
     for k in range(1, 8):
         total += wz[k].astype(F32)
     high, low = halves(total)
-    gi_ref[...] = -three(high, low, inv_hi[...], inv_lo[...], nt)
+    gio[...] = -three(high, low, inv_hi[...], inv_lo[...], nt)
+    out_gi = pltpu.make_async_copy(gio, gi_ref, lsem.at[13])
+    out_gi.start()
 
     @pl.when(jnp.logical_not(is_root))
     def _():
@@ -399,6 +387,10 @@
 
     for copy in sent:
         copy.wait_send()
+    for k in range(8):
+        out_rows(k).wait()
+    out_gp.wait()
+    out_gi.wait()
 
 
 def per_device(panel, slab, cotangent, inverse):
@@ -412,27 +404,28 @@
             jax.ShapeDtypeStruct((32, 256), F32),
         ),
         in_specs=[pl.BlockSpec(memory_space=pltpu.HBM)] * 4,
-        out_specs=[pl.BlockSpec(memory_space=vmem)] * 3,
+        out_specs=[pl.BlockSpec(memory_space=pl.ANY)] * 3,
         scratch_shapes=[
             vmem((8, 32, 256), F32), vmem((256, 256), F32),
             vmem((256, 256), BF), vmem((256, 256), BF), vmem((256, 256), BF), vmem((256, 256), BF),
             vmem((256, 256), BF), vmem((256, 256), BF),
-            vmem((2048, 4, 256), BF), vmem((4, 2048, 256), BF), vmem((2048, 4, 256), BF),
+            vmem((2048, 4, 256), BF), vmem((2048, 1024), BF), vmem((2048, 4, 256), BF),
             vmem((8, 8, 32, 256), BF), vmem((8, 256, 256), BF),
             vmem((4, 8, 32, 256), BF), vmem((4, 256, 256), BF),
-            vmem((4, 256, 256), F32), vmem((256, 256), F32),
+            vmem((256, 1024), F32), vmem((4, 256, 256), BF), vmem((256, 256), F32),
             vmem((4, 256, 256), BF), vmem((4, 256, 256), BF),
             vmem((8, 32, 256), BF), vmem((8, 32, 256), BF),
             vmem((32, 256), BF), vmem((32, 256), BF),
-            vmem((2048, 256), BF), vmem((2048, 256), BF), vmem((4, 2, 32, 256), F32),
+            vmem((2048, 256), BF), vmem((4, 2, 32, 256), F32),
             vmem((8, 4, 2, 32, 256), BF), vmem((8, 4, 32, 256), BF),
             vmem((4, 8, 32, 256), BF), vmem((4, 8, 32, 256), BF),
             vmem((4, 32, 256), F32), vmem((4, 32, 256), F32), vmem((4, 32, 256), F32),
             vmem((4, 32, 256), BF), vmem((8, 32, 256), BF),
-            pltpu.SemaphoreType.DMA((N_SEM,)), pltpu.SemaphoreType.DMA((N_SEM,)), pltpu.SemaphoreType.DMA((4,)),
+            vmem((8, 32, 256), F32), vmem((32, 256), F32),
+            pltpu.SemaphoreType.DMA((N_SEM,)), pltpu.SemaphoreType.DMA((N_SEM,)), pltpu.SemaphoreType.DMA((14,)),
         ],
         compiler_params=pltpu.CompilerParams(
-            collective_id=0, has_side_effects=True, vmem_limit_bytes=48 << 20
+            collective_id=0, has_side_effects=True, vmem_limit_bytes=56 << 20
         ),
     )(strips, slab.reshape(2048, 4, 256), cotangent.reshape(2048, 4, 256), inverse)
     return (

time: 59.2 us -> 53.9 us (0.910)
  Pallas kernels: 52.7 us -> 45.7 us
  local copies, waits for them, and re-layouts: 5.22 us -> 7.01 us
    pallas_call x1, Pallas kernels: 52.7 us -> 45.7 us  [per_device(): pl.pallas_call(kernel, out_shape=(jax.ShapeDtypeStruct((2048, 4, 256), BF...]
    unnamed x7, local copies, waits for them, and re-layouts: 5.22 us -> 7.01 us
where the time goes in v3:
time: 53.9 us; the launch traced here: 53.3 us
  Pallas kernels  45.7 us (85%)
  local copies, waits for them, and re-layouts  7.01 us (13%)
  between operations  0.66 us (1%)
    pallas_call x1, Pallas kernels, per_device(): pl.pallas_call(kernel, out_shape=(jax.ShapeDtypeStruct((2048, 4, 256), BF...  45.7 us
    unnamed x7, local copies, waits for them, and re-layouts  7.01 us

profile of v3, /device:TPU:6, one launch (start us, length us, event | category | flops | bytes accessed | tf_op | source)
XLA Modules:
  0.0 53.3 jit_solution(13480198907600995571)
XLA Ops:
  0.6 45.7 %shard_map.67 = (bf16[2048,4,256]{2,1,0:T(4,128)(2,1)}, f32[8,32,256]{2,1,0:T(8,128)}, f32[32,256]{1,0:T(8,128)}) custom-call(f32[8,32,256]{2,1,0:T(8,128)} %bitcast.17, bf16[2048,4,256]{2,1,0:T(4,128)(2,1)} %bitcast.14, bf16[2048,4,256]{2,1,0:T(4,128)(2,1)} %bitcast.15, f32[256,256]{1,0:T(8,128)} %inv_ref.1), custom_call_target="tpu_custom_call" | custom-call | tf_op jit(solution)/shard_map/pallas_call | solution.py:399
  46.3 0.0 copy-start
  46.3 0.0 copy-start.1
  46.3 5.7 %copy.12 = bf16[8,1,256,4,1,256]{5,3,4,2,1,0:T(4,128)(2,1)} copy(bf16[8,1,256,4,1,256]{5,3,4,2,1,0:T(4,128)(2,1)} %bitcast.16) | data formatting | bytes 8388608
  52.0 0.0 copy-done
  52.0 0.7 %copy.13 = f32[8,1,256,32]{2,3,1,0:T(8,128)} copy(f32[8,1,256,32]{2,3,1,0:T(8,128)S(1)} %bitcast.18) | data formatting | bytes 524288
  52.7 0.0 copy-done.1
  52.7 0.6 %copy.14 = f32[256,32]{0,1:T(8,128)} copy(f32[256,32]{0,1:T(8,128)S(1)} %bitcast.19) | data formatting | bytes 65536
Async XLA Ops:
  46.3 5.7 %copy-start = (f32[8,32,256]{2,1,0:T(8,128)S(1)}, f32[8,32,256]{2,1,0:T(8,128)}, u32[]{:S(2)}) copy-start(f32[8,32,256]{2,1,0:T(8,128)} %get-tuple-element.7) | copy-start | bytes 786436
  46.3 6.4 %copy-start.1 = (f32[32,256]{1,0:T(8,128)S(1)}, f32[32,256]{1,0:T(8,128)}, u32[]{:S(2)}) copy-start(f32[32,256]{1,0:T(8,128)} %get-tuple-element.8) | copy-start | bytes 98308

commit v4 on v3

--- a/solution.py
+++ b/solution.py
@@ -10,7 +10,7 @@
 MESH = pl.DeviceIdType.MESH
 
 
-S_A1, S_A2, S_B1, S_B2, S_B3 = 0, 8, 16, 17, 25
+S_A1, S_A2, S_B2, S_B3 = 0, 8, 17, 25
 S_E1, S_E2, S_E3 = 29, 37, 45
 S_D1, S_D2, S_WC, S_WX, S_WY, S_WZ = 46, 48, 56, 57, 61, 65
 N_SEM = 73
@@ -97,9 +97,12 @@
     for d in range(1, 8):
         hello(row_z(d), col)
 
+    for d in range(1, 8):
+        hello(mirror, (col + d) % 8)
+
     @pl.when(jnp.logical_not(is_root))
     def _():
-        hello(mirror, z)
+        hello(mirror, col)
 
     in_panel.wait()
     for k in range(8):
@@ -115,13 +118,17 @@
     t_high, t_low = halves(inv[...].T)
     k_hi[...], k_lo[...] = halves(three(t_high, t_low, high, low, nn))
 
-    pl.semaphore_wait(barrier, 15 - is_root.astype(jnp.int32))
-
-    b1 = remote(pt.at[0, col], tp.at[y, col], S_B1, S_B1, mirror, z)
+    pl.semaphore_wait(barrier, 22 - is_root.astype(jnp.int32))
+
+    def strip_to(d):
+        return remote(pt.at[0, col], tp.at[y, col], S_B2 + d, S_B2 + col, row_z(d), z)
+
+    for d in (1, 7, 2, 6, 3, 5, 4):
+        strip_to(d).start()
 
     @pl.when(jnp.logical_not(is_root))
     def _():
-        b1.start()
+        strip_to(0).start()
 
     @pl.when(is_root)
     def _():
@@ -146,8 +153,14 @@
             remote(tp.at[y, piece], tp.at[y, piece], S_B3 + d, S_B3 + d, row_y(d), col).start()
 
     def piece_from(d):
-        origin = (z + 8 - d) % 8
-        arrived(tp.at[y, origin], S_B2 + d)
+        origin = (col + d) % 8
+        if d == 0:
+
+            @pl.when(jnp.logical_not(is_root))
+            def _():
+                arrived(tp.at[y, origin], S_B2 + origin)
+        else:
+            arrived(tp.at[y, origin], S_B2 + origin)
         to_other_y(origin)
 
     in_cot.wait()
@@ -159,32 +172,29 @@
             gs[pl.ds(t * 64, 64), j * 256 : (j + 1) * 256] = moved[j * 64 : (j + 1) * 64]
         return carry
 
-    @pl.when(jnp.logical_not(is_root))
-    def _():
-        arrived(tp.at[y, z], S_B1)
-
-    for d in (4, 3, 5, 2, 6, 1, 7):
-        send(tp.at[y, z], tp.at[y, z], S_B2 + d, row_z(d), col)
-    to_other_y(z)
-
-    lax.fori_loop(0, 4, split_columns, 0, unroll=2)
+    def split(t0, t1):
+        lax.fori_loop(t0, t1, split_columns, 0, unroll=2)
+
+    split(0, 8)
+    piece_from(0)
+    piece_from(1)
+    piece_from(7)
     pass_on(0, 1)
     pass_on(0, 3)
-    piece_from(1)
-    piece_from(7)
-    lax.fori_loop(4, 8, split_columns, 0, unroll=2)
-    pass_on(0, 2)
+    split(8, 12)
     piece_from(2)
     piece_from(6)
-    lax.fori_loop(8, 14, split_columns, 0, unroll=2)
+    pass_on(0, 2)
+    split(12, 16)
+    piece_from(3)
+    piece_from(5)
+    piece_from(4)
+    split(16, 20)
     pass_on(1, 1)
     pass_on(1, 3)
-    piece_from(3)
-    piece_from(5)
-    lax.fori_loop(14, 18, split_columns, 0, unroll=2)
-    piece_from(4)
+    split(20, 26)
     pass_on(1, 2)
-    lax.fori_loop(18, 32, split_columns, 0, unroll=2)
+    split(26, 32)
 
     def panel_half(h):
         arrived(half(h, twin), S_A1 + 4 * h)
@@ -374,8 +384,11 @@
 
     @pl.when(jnp.logical_not(is_root))
     def _():
-        b1.wait_send()
+        strip_to(0).wait_send()
         e3_out.wait_send()
+
+    for d in range(1, 8):
+        strip_to(d).wait_send()
 
     for d in range(1, 4):
         remote(tp.at[y], tp.at[y], S_B3 + d, S_B3 + d, row_y(d), col).wait_send()
@@ -425,7 +438,7 @@
             pltpu.SemaphoreType.DMA((N_SEM,)), pltpu.SemaphoreType.DMA((N_SEM,)), pltpu.SemaphoreType.DMA((14,)),
         ],
         compiler_params=pltpu.CompilerParams(
-            collective_id=0, has_side_effects=True, vmem_limit_bytes=56 << 20
+            collective_id=0, has_side_effects=True, vmem_limit_bytes=48 << 20
         ),
     )(strips, slab.reshape(2048, 4, 256), cotangent.reshape(2048, 4, 256), inverse)
     return (

time: 53.9 us -> 49.6 us (0.920)
  Pallas kernels: 45.7 us -> 42.8 us
  local copies, waits for them, and re-layouts: 7.01 us -> 5.22 us
    pallas_call x1, Pallas kernels: 45.7 us -> 42.8 us  [per_device(): pl.pallas_call(kernel, out_shape=(jax.ShapeDtypeStruct((2048, 4, 256), BF...]
    unnamed x7, local copies, waits for them, and re-layouts: 7.01 us -> 5.22 us
where the time goes in v4:
time: 49.6 us; the launch traced here: 48.7 us
  Pallas kernels  42.8 us (86%)
  local copies, waits for them, and re-layouts  5.22 us (11%)
  between operations  0.65 us (1%)
    pallas_call x1, Pallas kernels, per_device(): pl.pallas_call(kernel, out_shape=(jax.ShapeDtypeStruct((2048, 4, 256), BF...  42.8 us
    unnamed x7, local copies, waits for them, and re-layouts  5.22 us

profile of v4, /device:TPU:6, one launch (start us, length us, event | category | flops | bytes accessed | tf_op | source)
XLA Modules:
  0.0 48.7 jit_solution(11080191433261018109)
XLA Ops:
  0.6 0.0 copy-start
  0.6 0.9 %copy-done = f32[8,1,256,32]{2,3,1,0:T(8,128)S(1)} copy-done((f32[8,1,256,32]{2,3,1,0:T(8,128)S(1)}, f32[8,1,256,32]{2,3,1,0:T(8,128)}, u32[]{:S(2)}) %copy-start) | copy-done | bytes 262168
  1.6 0.0 copy-start.1
  1.6 0.9 %copy-done.1 = f32[256,256]{1,0:T(8,128)S(1)} copy-done((f32[256,256]{1,0:T(8,128)S(1)}, f32[256,256]{1,0:T(8,128)}, u32[]{:S(2)}) %copy-start.1) | copy-done | bytes 262168
  2.5 42.8 %shard_map.67 = (bf16[2048,4,256]{2,1,0:T(4,128)(2,1)S(1)}, f32[8,32,256]{2,1,0:T(8,128)S(1)}, f32[32,256]{1,0:T(8,128)S(1)}) custom-call(f32[8,32,256]{2,1,0:T(8,128)S(1)} %bitcast.15, bf16[2048,4,256]{2,1,0:T(4,128)(2,1)} %bitcast.18, bf16[2048,4,256]{2,1,0:T(4,128)(2,1)} %bitcast.19, f32[256,256]{1,0:T(8,128)S(1)} %copy-done.1), custom_call_target="tpu_custom_call" | custom-call | tf_op jit(solution)/shard_map/pallas_call | solution.py:412
  45.3 2.0 %copy.12 = bf16[8,1,256,4,1,256]{5,3,4,2,1,0:T(4,128)(2,1)} copy(bf16[8,1,256,4,1,256]{5,3,4,2,1,0:T(4,128)(2,1)S(1)} %bitcast.14) | data formatting | bytes 8388608
  47.3 0.7 %copy.13 = f32[8,1,256,32]{2,3,1,0:T(8,128)} copy(f32[8,1,256,32]{2,3,1,0:T(8,128)S(1)} %bitcast.16) | data formatting | bytes 524288
  48.0 0.6 %copy.14 = f32[256,32]{0,1:T(8,128)} copy(f32[256,32]{0,1:T(8,128)S(1)} %bitcast.17) | data formatting | bytes 65536
Async XLA Ops:
  0.6 1.0 %copy-start = (f32[8,1,256,32]{2,3,1,0:T(8,128)S(1)}, f32[8,1,256,32]{2,3,1,0:T(8,128)}, u32[]{:S(2)}) copy-start(f32[8,1,256,32]{2,3,1,0:T(8,128)} %param.4) | copy-start | bytes 786436
  1.6 0.9 %copy-start.1 = (f32[256,256]{1,0:T(8,128)S(1)}, f32[256,256]{1,0:T(8,128)}, u32[]{:S(2)}) copy-start(f32[256,256]{1,0:T(8,128)} %inv_ref.1) | copy-start | bytes 786436

commit v5 on v4

--- a/solution.py
+++ b/solution.py
@@ -215,11 +215,15 @@
         q_bf[j] = total
         return nn(k_hi[...], total) + nn(k_lo[...], total)
 
+    def column_half(d, h):
+        rows = pl.ds(128 * h, 128)
+        send(n_send.at[d, rows], e1.at[d, rows], S_E1 + 4 * h + d, row_y(d), col)
+
     for d in (2, 1, 3):
         n_send[d] = column_tile((y + d) % 4).astype(BF)
-        for h in range(2):
-            rows = pl.ds(128 * h, 128)
-            send(n_send.at[d, rows], e1.at[d, rows], S_E1 + 4 * h + d, row_y(d), col)
+        column_half(d, 0)
+    for d in (2, 1, 3):
+        column_half(d, 1)
     n_own[...] = column_tile(y)
 
     for d in range(1, 4):
@@ -233,10 +237,10 @@
         r_bf[rows, :] = nt(gs[rows, :], top_columns()).astype(BF)
         return carry
 
+    q_all = jnp.concatenate([q_bf[j] for j in range(4)], axis=1)
+    w[...] = (nt(q_all, top_columns()) + nt(top_columns(), q_all)).reshape(4, 2, 32, 256)
+    send(w.at[:, 1 - core], wd, S_WC, row, twin)
     lax.fori_loop(0, 4, column_sum, 0)
-    q_all = jnp.concatenate([q_bf[j] for j in range(4)], axis=1)
-    w[...] = (nn(panel_rows(0, 8), r_bf[...]) + nt(top_columns(), q_all)).reshape(4, 2, 32, 256)
-    send(w.at[:, 1 - core], wd, S_WC, row, twin)
 
     def k_tile(k, carry):
         rows = pl.ds(pl.multiple_of(k * 256, 256), 256)
@@ -270,19 +274,17 @@
             def _():
                 remote(e2s.at[other], e2r.at[z], S_E2 + other, S_E2 + z, y * 8 + other, col).start()
 
-    lax.fori_loop(0, 4, k_tile, 0)
-    core_half(0)
-
     arrived(wd, S_WC)
     wc[...] = w[:, core] + wd[...]
     for d in (2, 1, 3):
         send(wc.at[x_at(d)], wx.at[d], S_WX + d, row, col_at(d))
 
+    lax.fori_loop(0, 4, k_tile, 0)
+    core_half(0)
+    strips_out(0)
     lax.fori_loop(4, 8, k_tile, 0)
     core_half(1)
     join(0)
-    strips_out(0)
-    join(1)
     strips_out(1)
 
     for d in range(1, 4):
@@ -291,6 +293,7 @@
     wy[y] = total
     for d in (2, 1, 3):
         send(wy.at[y], wy.at[y], S_WY + d, row_y(d), col)
+    join(1)
 
     def top_tile(j, carry):
         tile = tp[j].reshape(256, 256)
@@ -303,7 +306,7 @@
         return carry
 
     lax.fori_loop(0, 4, top_tile, 0)
-    lax.fori_loop(0, 4, factor_tile, 0)
+    lax.fori_loop(0, 8, factor_tile, 0)
 
     for d in range(1, 4):
         arrived(wy.at[(y + 4 - d) % 4], S_WY + d)
@@ -328,7 +331,6 @@
     def _():
         e3_out.start()
 
-    lax.fori_loop(4, 8, factor_tile, 0)
     in_slab.wait()
 
     def out_rows(k):
@@ -440,7 +442,7 @@
         compiler_params=pltpu.CompilerParams(
             collective_id=0, has_side_effects=True, vmem_limit_bytes=48 << 20
         ),
-    )(strips, slab.reshape(2048, 4, 256), cotangent.reshape(2048, 4, 256), inverse)
+    )(pltpu.with_memory_space_constraint(strips, pltpu.HBM), slab.reshape(2048, 4, 256), cotangent.reshape(2048, 4, 256), pltpu.with_memory_space_constraint(inverse, pltpu.HBM))
     return (
         updated.reshape(slab.shape),
         jnp.transpose(grad_panel, (0, 2, 1)).reshape(panel.shape),

time: 49.6 us -> 47.5 us (0.958)
  local copies, waits for them, and re-layouts: 5.22 us -> 3.33 us
    unnamed x7 -> x3, local copies, waits for them, and re-layouts: 5.22 us -> 3.33 us
where the time goes in v5:
time: 47.5 us; the launch traced here: 47 us
  Pallas kernels  43 us (91%)
  local copies, waits for them, and re-layouts  3.33 us (7%)
  between operations  0.64 us (1%)
    pallas_call x1, Pallas kernels, per_device(): pl.pallas_call(kernel, out_shape=(jax.ShapeDtypeStruct((2048, 4, 256), BF...  43 us
    unnamed x3, local copies, waits for them, and re-layouts  3.33 us

profile of v5, /device:TPU:6, one launch (start us, length us, event | category | flops | bytes accessed | tf_op | source)
XLA Modules:
  0.0 47.0 jit_solution(14859831352128514285)
XLA Ops:
  0.6 43.0 %shard_map.67 = (bf16[2048,4,256]{2,1,0:T(4,128)(2,1)S(1)}, f32[8,32,256]{2,1,0:T(8,128)S(1)}, f32[32,256]{1,0:T(8,128)S(1)}) custom-call(f32[8,32,256]{2,1,0:T(8,128)} %bitcast.19, bf16[2048,4,256]{2,1,0:T(4,128)(2,1)} %bitcast.17, bf16[2048,4,256]{2,1,0:T(4,128)(2,1)} %bitcast.18, f32[256,256]{1,0:T(8,128)} %inv_ref.1), custom_call_target="tpu_custom_call" | custom-call | tf_op jit(solution)/shard_map/pallas_call | solution.py:414
  43.6 2.0 %copy.12 = bf16[8,1,256,4,1,256]{5,3,4,2,1,0:T(4,128)(2,1)} copy(bf16[8,1,256,4,1,256]{5,3,4,2,1,0:T(4,128)(2,1)S(1)} %bitcast.14) | data formatting | bytes 8388608
  45.7 0.7 %copy.13 = f32[8,1,256,32]{2,3,1,0:T(8,128)} copy(f32[8,1,256,32]{2,3,1,0:T(8,128)S(1)} %bitcast.15) | data formatting | bytes 524288
  46.4 0.6 %copy.14 = f32[256,32]{0,1:T(8,128)} copy(f32[256,32]{0,1:T(8,128)S(1)} %bitcast.16) | data formatting | bytes 65536

commit v6 on v5

--- a/solution.py
+++ b/solution.py
@@ -11,7 +11,7 @@
 
 
 S_A1, S_A2, S_B2, S_B3 = 0, 8, 17, 25
-S_E1, S_E2, S_E3 = 29, 37, 45
+S_E1, S_E2 = 29, 37
 S_D1, S_D2, S_WC, S_WX, S_WY, S_WZ = 46, 48, 56, 57, 61, 65
 N_SEM = 73
 
@@ -37,7 +37,7 @@
     panel_ref, slab_ref, cot_ref, inv_ref, upd_ref, gp_ref, gi_ref,
     strip, inv, inv_hi, inv_lo, k_hi, k_lo, perm, permt,
     graw, gs, sraw, pt, fn, tp, topt,
-    q_sum, q_bf, n_own, n_send, e1, e2s, e2r, e3s, e3,
+    q_sum, q_bf, n_own, n_send, e1, e2s, e2r,
     r_bf, w, mst, d1, cmb, d2, wd, wc, wx, wy, wz, gpo, gio,
     ssem, rsem, lsem,
 ):
@@ -260,19 +260,24 @@
             part = pl.ds(4 * h, 4)
             send(cmb.at[x_at(d), part], d2.at[d, part], S_D2 + 4 * h + d, row, col_at(d))
 
+    def strip_home(other):
+        return remote(e2s.at[other], e2r.at[z], S_E2 + other, S_E2 + z, mirror, other)
+
+    def leaves(other):
+        return jnp.logical_or(z != col, col != other)
+
     def strips_out(h):
         rows = pl.ds(128 * h, 128)
         total = n_own[rows, :]
         for d in range(1, 4):
             arrived(e1.at[d, rows], S_E1 + 4 * h + d)
             total += e1[d, rows, :].astype(F32)
-        n_own[rows, :] = total
         e2s[pl.ds(4 * h, 4)] = total.reshape(4, 32, 256).astype(BF)
         for other in range(4 * h, 4 * h + 4):
 
-            @pl.when(z != other)
+            @pl.when(leaves(other))
             def _():
-                remote(e2s.at[other], e2r.at[z], S_E2 + other, S_E2 + z, y * 8 + other, col).start()
+                strip_home(other).start()
 
     arrived(wd, S_WC)
     wc[...] = w[:, core] + wd[...]
@@ -281,18 +286,17 @@
 
     lax.fori_loop(0, 4, k_tile, 0)
     core_half(0)
-    strips_out(0)
     lax.fori_loop(4, 8, k_tile, 0)
     core_half(1)
     join(0)
-    strips_out(1)
-
+    strips_out(0)
     for d in range(1, 4):
         arrived(wx.at[d], S_WX + d)
     total = (wc[x] + wx[1] + wx[2] + wx[3]).astype(BF)
     wy[y] = total
     for d in (2, 1, 3):
         send(wy.at[y], wy.at[y], S_WY + d, row_y(d), col)
+    strips_out(1)
     join(1)
 
     def top_tile(j, carry):
@@ -316,20 +320,6 @@
     wz[z] = total.astype(BF)
     for d in (4, 3, 5, 2, 6, 1, 7):
         send(wz.at[z], wz.at[z], S_WZ + d, row_z(d), col)
-
-    for d in range(1, 8):
-        origin = (z + 8 - d) % 8
-        arrived(e2r.at[origin], S_E2 + origin)
-    e2r[z] = jnp.zeros((32, 256), BF)
-    total = n_own[pl.ds(pl.multiple_of(z * 32, 32), 32), :]
-    for k in range(8):
-        total += e2r[k].astype(F32)
-    e3s[...] = total.astype(BF)
-    e3_out = remote(e3s, e3, S_E3, S_E3, mirror, z)
-
-    @pl.when(jnp.logical_not(is_root))
-    def _():
-        e3_out.start()
 
     in_slab.wait()
 
@@ -359,15 +349,21 @@
             value += d2[d, k].astype(F32)
         gpo[k] = -value
 
+    for d in range(1, 8):
+        origin = (z + d) % 8
+        arrived(e2r.at[origin], S_E2 + origin)
+
     @pl.when(is_root)
     def _():
-        e3[...] = e3s[...]
+        e2r[z] = e2s[col]
 
     @pl.when(jnp.logical_not(is_root))
     def _():
-        arrived(e3, S_E3)
-
-    value = mst[0, x, core].astype(F32) + d1[0, x].astype(F32) + e3[...].astype(F32)
+        arrived(e2r.at[z], S_E2 + z)
+
+    value = mst[0, x, core].astype(F32) + d1[0, x].astype(F32)
+    for origin in range(8):
+        value += e2r[origin].astype(F32)
     for d in range(1, 4):
         value += d2[d, 0].astype(F32)
     gpo[0] = -value
@@ -387,7 +383,6 @@
     @pl.when(jnp.logical_not(is_root))
     def _():
         strip_to(0).wait_send()
-        e3_out.wait_send()
 
     for d in range(1, 8):
         strip_to(d).wait_send()
@@ -396,9 +391,9 @@
         remote(tp.at[y], tp.at[y], S_B3 + d, S_B3 + d, row_y(d), col).wait_send()
     for other in range(8):
 
-        @pl.when(z != other)
+        @pl.when(leaves(other))
         def _():
-            remote(e2s.at[other], e2r.at[z], S_E2 + other, S_E2 + z, y * 8 + other, col).wait_send()
+            strip_home(other).wait_send()
 
     for copy in sent:
         copy.wait_send()
@@ -430,7 +425,6 @@
             vmem((256, 1024), F32), vmem((4, 256, 256), BF), vmem((256, 256), F32),
             vmem((4, 256, 256), BF), vmem((4, 256, 256), BF),
             vmem((8, 32, 256), BF), vmem((8, 32, 256), BF),
-            vmem((32, 256), BF), vmem((32, 256), BF),
             vmem((2048, 256), BF), vmem((4, 2, 32, 256), F32),
             vmem((8, 4, 2, 32, 256), BF), vmem((8, 4, 32, 256), BF),
             vmem((4, 8, 32, 256), BF), vmem((4, 8, 32, 256), BF),

time: 47.5 us -> 48.8 us (1.027)
  the two profiles are of different devices: /device:TPU:6 before, /device:TPU:1 now
where the time goes in v6:
time: 48.8 us; the launch traced here: 48.7 us
  Pallas kernels  44.8 us (92%)
  local copies, waits for them, and re-layouts  3.33 us (7%)
  between operations  0.64 us (1%)
    pallas_call x1, Pallas kernels, per_device(): pl.pallas_call(kernel, out_shape=(jax.ShapeDtypeStruct((2048, 4, 256), BF...  44.8 us
    unnamed x3, local copies, waits for them, and re-layouts  3.33 us

profile of v6, /device:TPU:1, one launch (start us, length us, event | category | flops | bytes accessed | tf_op | source)
XLA Modules:
  0.0 48.7 jit_solution(3982274198661900619)
XLA Ops:
  0.6 44.8 %shard_map.67 = (bf16[2048,4,256]{2,1,0:T(4,128)(2,1)S(1)}, f32[8,32,256]{2,1,0:T(8,128)S(1)}, f32[32,256]{1,0:T(8,128)S(1)}) custom-call(f32[8,32,256]{2,1,0:T(8,128)} %bitcast.19, bf16[2048,4,256]{2,1,0:T(4,128)(2,1)} %bitcast.17, bf16[2048,4,256]{2,1,0:T(4,128)(2,1)} %bitcast.18, f32[256,256]{1,0:T(8,128)} %inv_ref.1), custom_call_target="tpu_custom_call" | custom-call | tf_op jit(solution)/shard_map/pallas_call | solution.py:409
  45.4 2.0 %copy.12 = bf16[8,1,256,4,1,256]{5,3,4,2,1,0:T(4,128)(2,1)} copy(bf16[8,1,256,4,1,256]{5,3,4,2,1,0:T(4,128)(2,1)S(1)} %bitcast.14) | data formatting | bytes 8388608
  47.4 0.7 %copy.13 = f32[8,1,256,32]{2,3,1,0:T(8,128)} copy(f32[8,1,256,32]{2,3,1,0:T(8,128)S(1)} %bitcast.15) | data formatting | bytes 524288
  48.1 0.6 %copy.14 = f32[256,32]{0,1:T(8,128)} copy(f32[256,32]{0,1:T(8,128)S(1)} %bitcast.16) | data formatting | bytes 65536

commit v7 on v5

--- a/solution.py
+++ b/solution.py
@@ -281,18 +281,17 @@
 
     lax.fori_loop(0, 4, k_tile, 0)
     core_half(0)
-    strips_out(0)
     lax.fori_loop(4, 8, k_tile, 0)
     core_half(1)
     join(0)
-    strips_out(1)
-
+    strips_out(0)
     for d in range(1, 4):
         arrived(wx.at[d], S_WX + d)
     total = (wc[x] + wx[1] + wx[2] + wx[3]).astype(BF)
     wy[y] = total
     for d in (2, 1, 3):
         send(wy.at[y], wy.at[y], S_WY + d, row_y(d), col)
+    strips_out(1)
     join(1)
 
     def top_tile(j, carry):

time: 47.5 us -> 47.2 us (level)
  no operation moved by 1% of the time
where the time goes in v7:
time: 47.2 us; the launch traced here: 47.1 us
  Pallas kernels  43.2 us (92%)
  local copies, waits for them, and re-layouts  3.33 us (7%)
  between operations  0.64 us (1%)
    pallas_call x1, Pallas kernels, per_device(): pl.pallas_call(kernel, out_shape=(jax.ShapeDtypeStruct((2048, 4, 256), BF...  43.2 us
    unnamed x3, local copies, waits for them, and re-layouts  3.33 us

profile of v7, /device:TPU:6, one launch (start us, length us, event | category | flops | bytes accessed | tf_op | source)
XLA Modules:
  0.0 47.1 jit_solution(12162272933839994103)
XLA Ops:
  0.6 43.2 %shard_map.67 = (bf16[2048,4,256]{2,1,0:T(4,128)(2,1)S(1)}, f32[8,32,256]{2,1,0:T(8,128)S(1)}, f32[32,256]{1,0:T(8,128)S(1)}) custom-call(f32[8,32,256]{2,1,0:T(8,128)} %bitcast.19, bf16[2048,4,256]{2,1,0:T(4,128)(2,1)} %bitcast.17, bf16[2048,4,256]{2,1,0:T(4,128)(2,1)} %bitcast.18, f32[256,256]{1,0:T(8,128)} %inv_ref.1), custom_call_target="tpu_custom_call" | custom-call | tf_op jit(solution)/shard_map/pallas_call | solution.py:413
  43.8 2.0 %copy.12 = bf16[8,1,256,4,1,256]{5,3,4,2,1,0:T(4,128)(2,1)} copy(bf16[8,1,256,4,1,256]{5,3,4,2,1,0:T(4,128)(2,1)S(1)} %bitcast.14) | data formatting | bytes 8388608
  45.8 0.7 %copy.13 = f32[8,1,256,32]{2,3,1,0:T(8,128)} copy(f32[8,1,256,32]{2,3,1,0:T(8,128)S(1)} %bitcast.15) | data formatting | bytes 524288
  46.5 0.6 %copy.14 = f32[256,32]{0,1:T(8,128)} copy(f32[256,32]{0,1:T(8,128)S(1)} %bitcast.16) | data formatting | bytes 65536
